TPU v7x, 32 devices: a whole 2x2x4 slice. The times are simulated.
32 devices in a mesh: gx: 8 (over z, core), gy: 4 (over y, x).
Axes of the slice: x: 2, y: 2, z: 4, core: 2. Of those that a mesh axis runs over, the one named last changes fastest.
Arguments:
- density: float32 [128, 192, 128], P('gx', 'gy'), may hold values from -6 to 6
- momenta: float32 [3, 128, 192, 128], P(None, 'gx', 'gy'), may hold values from -6 to 6
- smooth_taps: float32 [33], replicated, may hold values from -1 to 1
- deriv_taps: float32 [33], replicated, may hold values from -1 to 1
- kick_step: float32 [], replicated, may hold values from 0.5 to 1.5
Outputs:
- kicked: float32 [3, 128, 192, 128], P(None, 'gx', 'gy')
All inputs are finite; a program needn't handle non-finite values.
Results may differ from a plain program's by a relative error of at most 0.00007.
Values sent between devices are 32-bit elements; how exact they have to be, the bound alone decides.
No kernel may reach another device: no remote copies, remote signals or barrier semaphores. Data moves between devices by JAX's collectives and lax.ppermute only.
A program may use at most 64 MiB of HBM per device.

v0:
```python
import functools
import math

import jax
import jax.numpy as jnp
import ml_dtypes
import numpy as np
from jax import lax
from jax.experimental import pallas as pl
from jax.experimental.pallas import tpu as pltpu
from jax.sharding import PartitionSpec as P


FACTOR = 4
LANES = 128
CHUNK = 8
GROUP = 8
LONG_COUPLING = 16.0
VMEM = pl.BlockSpec(memory_space=pltpu.VMEM)
SMEM = pl.BlockSpec(memory_space=pltpu.SMEM)
HBM = pl.BlockSpec(memory_space=pltpu.HBM)
DMA = pltpu.SemaphoreType.DMA


def real_basis(count):
    places = np.arange(count, dtype=np.float64)
    rows, waves = [np.full(count, 1.0 / math.sqrt(count))], [0]
    for wave in range(1, (count + 1) // 2):
        phase = 2.0 * math.pi * wave * places / count
        rows += [math.sqrt(2.0 / count) * np.cos(phase), math.sqrt(2.0 / count) * np.sin(phase)]
        waves += [wave, wave]
    if count % 2 == 0:
        rows.append(np.cos(math.pi * places) / math.sqrt(count))
        waves.append(count // 2)
    return np.stack(rows), np.array(waves)


def centred(basis):
    return 0.5 * (np.roll(basis, -1, 1) - np.roll(basis, 1, 1))


def eigenvalues(waves, count):
    return 2.0 - 2.0 * np.cos(2.0 * math.pi * waves / count)


def split_table(table, axis):
    table = np.asarray(table, dtype=np.float32)
    high = table.astype(ml_dtypes.bfloat16)
    low = (table - high.astype(np.float32)).astype(ml_dtypes.bfloat16)
    return np.concatenate([high, low, high], axis)


def split(values):
    high = values.astype(jnp.bfloat16)
    low = (values - high.astype(jnp.float32)).astype(jnp.bfloat16)
    return high, low


def tripled(values, axis):
    high, low = split(values)
    return jnp.concatenate([high, high, low], axis=axis)


def dot(left, right):
    return jnp.dot(left, right, preferred_element_type=jnp.float32)


def prepare_kernel(density_far, pool_far, density, head, tail, coarse, pool_table, pooled, sems):
    rows, cols, _ = density.shape
    radius = head.shape[0]
    groups, lines = rows // FACTOR, cols // FACTOR
    copies = [
        pltpu.make_async_copy(
            density_far.at[pl.ds(FACTOR * group, FACTOR)], density.at[pl.ds(FACTOR * group, FACTOR)], sems.at[group]
        )
        for group in range(groups)
    ]
    copies.append(pltpu.make_async_copy(pool_far, pool_table, sems.at[groups]))
    for copy in copies:
        copy.start()
    for group in range(groups):
        copies[group].wait()
        total = density[FACTOR * group]
        for step in range(1, FACTOR):
            total = total + density[FACTOR * group + step]
        pooled[group * cols : (group + 1) * cols, :] = total
    parts = []
    for group in range(groups):
        total = pooled[pl.ds(group * cols, lines, stride=FACTOR), :]
        for step in range(1, FACTOR):
            total = total + pooled[pl.ds(group * cols + step, lines, stride=FACTOR), :]
        parts.append(total)
    copies[groups].wait()
    waves = dot(tripled(jnp.concatenate(parts, axis=0), 1), pool_table[...])
    lane_group = lax.broadcasted_iota(jnp.int32, (lines, LANES), 1) // (LANES // groups)
    result = waves[:lines]
    for group in range(1, groups):
        result = jnp.where(lane_group == group, waves[group * lines : (group + 1) * lines], result)
    result = jnp.concatenate([result, jnp.zeros((coarse.shape[1] - lines, LANES), jnp.float32)], axis=0)

    def spread_out(copy, carry):
        coarse[copy] = result
        return carry

    lax.fori_loop(0, coarse.shape[0], spread_out, 0, unroll=coarse.shape[0] <= 64)
    for col in range(radius):
        head[col] = density[:, col, :]
        tail[col] = density[:, cols - radius + col, :]


def band_rows(rows, cols, depth, radius):
    sizes = {
        "x": (2 * rows, 9 * rows), "own": (2 * cols, 3 * cols), "sides": (4 * radius, 6 * radius),
        "smooth": (3 * depth, depth), "deriv": (3 * depth, depth),
    }
    places, start = {}, 0
    for name, (height, width) in sizes.items():
        places[name] = (start, start + height, width)
        start += height
    return places


def band(bands, places, name):
    start, stop, width = places[name]
    return bands[start:stop, :width]


def bands_kernel(smooth_far, deriv_far, step, bands, scale, smooth, deriv, sems, *, rows, cols, depth, radius):
    copies = [
        pltpu.make_async_copy(smooth_far, smooth, sems.at[0]), pltpu.make_async_copy(deriv_far, deriv, sems.at[1]),
    ]
    for copy in copies:
        copy.start()
    scale[...] = jnp.full(scale.shape, step[...], jnp.float32)
    for copy in copies:
        copy.wait()
    taps = 2 * radius + 1
    odd = lax.axis_index("core")
    at = band_rows(rows, cols, depth, radius)

    def banded(offset):
        pair = [jnp.zeros(offset.shape, jnp.float32)] * 2
        for tap in range(taps):
            here = offset == tap
            pair = [jnp.where(here, w[tap], m) for w, m in zip((smooth, deriv), pair)]
        return pair

    def iotas(shape):
        return lax.broadcasted_iota(jnp.int32, shape, 0), lax.broadcasted_iota(jnp.int32, shape, 1)

    def left_factor(name, offset):
        high, low = split(jnp.concatenate(banded(offset), axis=0))
        start, stop, width = at[name]
        bands[start:stop, :width] = jnp.concatenate([high, low, high], axis=1)

    target, source = iotas((rows, 3 * rows))
    side = jnp.where(odd == 1, -1, 1)
    place = jnp.where(
        source < rows, source,
        jnp.where(source < 2 * rows, source - rows + side * rows, source - 2 * rows - side * rows),
    )
    left_factor("x", place - target + radius)

    target, source = iotas((cols, cols))
    left_factor("own", source - target + radius)
    target, source = iotas((2 * radius, 2 * radius))
    place = jnp.where(source < radius, source - radius, source - radius + cols)
    row = jnp.where(target < radius, target, target - 2 * radius + cols)
    left_factor("sides", place - row + radius)

    source, target = iotas((depth, depth))
    offset = source - target + radius
    offset = jnp.where(offset < 0, offset + depth, offset)
    offset = jnp.where(offset >= depth, offset - depth, offset)
    for name, matrix in zip(("smooth", "deriv"), banded(offset)):
        high, low = split(matrix)
        start, stop, width = at[name]
        bands[start:stop, :width] = jnp.concatenate([high, low, high], axis=0)


def solve_kernel(
    blocks, beside_blocks, spread, tables, own_tables, back_z, forward, inverse, force,
    gathered, turned, back, columns, *, lines,
):
    core = lax.axis_index("core")
    fine = force.shape[2]
    groups = force.shape[1]
    quads = back.shape[0]
    whole_y = gathered.shape[0]
    parts = whole_y // lines
    count = 2 * blocks.shape[0] // parts
    width = LANES // FACTOR
    few = count <= CHUNK

    def spin_block(pair, carry):
        for side, source in enumerate((blocks, beside_blocks)):
            for part in range(parts):
                gathered[part * lines : (part + 1) * lines, :LANES] = source[pair * parts + part, :lines, :]
            values = gathered[:, :LANES]
            place = (2 * pair + (core if side == 0 else 1 - core)) * FACTOR
            for spin in range(FACTOR):
                turned[place + spin] = values if spin == 0 else pltpu.roll(values, LANES - spin * width, 1)
        return carry

    lax.fori_loop(0, count // 2, spin_block, 0, unroll=few)

    def chunk(step, carry):
        for at in range(CHUNK):
            place = (step * CHUNK + at) * count * FACTOR

            def term(index, total):
                return total + turned[index] * spread[pl.ds(place + index, 1), :]

            gathered[:, at * LANES : (at + 1) * LANES] = lax.fori_loop(
                0, count * FACTOR, term, jnp.zeros((whole_y, LANES), jnp.float32), unroll=True if few else 4
            )
        values = dot(forward[...], tripled(gathered[...], 0))
        own = tables[:whole_y, :]
        total = jnp.concatenate(
            [own + tables[pl.ds(whole_y + step * CHUNK + at, 1), :] for at in range(CHUNK)], axis=1
        )
        scale = jnp.where(total > 0.0, 1.0 / jnp.where(total > 0.0, total, 1.0), 0.0)
        result = dot(inverse[...], tripled(values * scale, 0))
        for at in range(CHUNK):
            back[step * CHUNK + at] = result[:, at * LANES : (at + 1) * LANES]
        return carry

    lax.fori_loop(0, quads // CHUNK, chunk, 0)

    for group in range(groups):
        def collect(index, totals):
            whole = back[index]
            value, slope = whole[:fine], whole[fine:]
            along = own_tables[pl.ds(index * 2 * groups + group, 1), :]
            along_slope = own_tables[pl.ds((index * 2 + 1) * groups + group, 1), :]
            return (
                totals[0] + value * along_slope, totals[1] + slope * along, totals[2] + value * along,
            )

        zero = jnp.zeros((fine, LANES), jnp.float32)
        totals = lax.fori_loop(0, quads, collect, (zero, zero, zero), unroll=few)
        for component in range(3):
            columns[component, group * fine : (group + 1) * fine, :] = totals[component]
    for component in range(3):
        result = dot(tripled(columns[component], 1), back_z[1 if component == 2 else 0])
        for group in range(groups):
            force[component, group] = result[group * fine : (group + 1) * fine]


def along_first(columns, matrix, out_smooth, out_deriv, wide):
    rows, depth = matrix.shape[0] // 2, LANES
    for start in range(0, len(columns), CHUNK):
        some = columns[start : start + CHUNK]
        stacked = jnp.concatenate(
            [tripled(jnp.concatenate(parts(), axis=0), 0) for _, parts in some], axis=1
        )
        result = dot(matrix, stacked)
        for at, (col, _) in enumerate(some):
            out_smooth[pl.ds(col, rows, stride=wide), :] = result[:rows, at * depth : (at + 1) * depth]
            out_deriv[pl.ds(col, rows, stride=wide), :] = result[rows:, at * depth : (at + 1) * depth]


def along_others(smooth_x, deriv_x, rows, wide, along_y, smooth_z, deriv_z):
    pieces = [[], [], []]
    count, depth = along_y.shape[0] // 2, LANES
    for row in rows:
        values = jnp.concatenate(
            [smooth_x[row * wide : (row + 1) * wide, :], deriv_x[row * wide : (row + 1) * wide, :]], axis=1
        )
        result = dot(along_y, tripled(values, 0))
        for at, piece in enumerate((result[:count, depth:], result[count:, :depth], result[:count, :depth])):
            pieces[at].append(tripled(piece, 1))
    smooth = dot(jnp.concatenate(pieces[0] + pieces[1], axis=0), smooth_z)
    deriv = dot(jnp.concatenate(pieces[2], axis=0), deriv_z)
    number = len(rows)
    return [
        [smooth[at * count : (at + 1) * count] for at in range(number)],
        [smooth[(number + at) * count : (number + at + 1) * count] for at in range(number)],
        [deriv[at * count : (at + 1) * count] for at in range(number)],
    ]


def inner_kernel(
    own, swapped, crossed, bands, momenta_far, scale_row,
    spread_far, tables_far, own_tables_far, back_z_far, forward_far, inverse_far,
    partial, spread, tables, own_tables, back_z, forward, inverse,
    smooth_x, deriv_x, momenta, sem, loads, *, group, radius
):
    gx, gy = 2 * lax.axis_index("pair") + lax.axis_index("core"), lax.axis_index("gy")
    loading = [
        pltpu.make_async_copy(source, target, loads.at[at])
        for at, (source, target) in enumerate((
            (spread_far, spread), (tables_far, tables), (own_tables_far.at[gx], own_tables), (back_z_far, back_z),
            (forward_far, forward), (inverse_far.at[gy], inverse),
        ))
    ]
    arriving = pltpu.make_async_copy(momenta_far, momenta, sem)
    arriving.start()
    for copy in loading:
        copy.start()
    rows, cols, depth = own.shape
    places = band_rows(rows, cols, depth, radius)
    along_x, own_y, smooth_z, deriv_z = [band(bands, places, n) for n in ("x", "own", "smooth", "deriv")]
    along_first(
        [(col, lambda col=col: [own[:, col, :], swapped[:, col, :], crossed[:, col, :]]) for col in range(cols)],
        along_x, smooth_x, deriv_x, cols,
    )
    arriving.wait()
    scale = scale_row[0:1, :]
    for start in range(0, rows, group):
        short = along_others(
            smooth_x, deriv_x, range(start, start + group), cols, own_y, smooth_z, deriv_z
        )
        for component in range(3):
            for at in range(group):
                partial[component, start + at] = momenta[component, start + at] + scale * short[component][at]
    for copy in loading:
        copy.wait()


def outer_kernel(
    left, right, beside_left, beside_right, cross_left, cross_right, bands, partial, scale_row, force,
    kicked, smooth_x, deriv_x, staged, sems, *, group,
):
    radius = left.shape[0]
    _, rows, cols, depth = partial.shape
    places = band_rows(rows, cols, depth, radius)
    along_x, sides_y, smooth_z, deriv_z = [band(bands, places, n) for n in ("x", "sides", "smooth", "deriv")]
    along_first(
        [(col, lambda col=col: [left[col], beside_left[col], cross_left[col]]) for col in range(radius)]
        + [
            (radius + col, lambda col=col: [right[col], beside_right[col], cross_right[col]])
            for col in range(radius)
        ],
        along_x, smooth_x, deriv_x, 2 * radius,
    )
    scale = scale_row[0:1, :]
    copies = []
    for start in range(0, rows, group):
        short = along_others(
            smooth_x, deriv_x, range(start, start + group), 2 * radius, sides_y, smooth_z, deriv_z
        )
        for component in range(3):
            for at in range(group):
                row = start + at
                far = force[component, row // FACTOR]
                base = partial[component, row]
                near = short[component][at]
                staged[component, row, :radius] = base[:radius] + scale * (near[:radius] + far[:radius])
                staged[component, row, radius : cols - radius] = (
                    base[radius : cols - radius] + scale * far[radius : cols - radius]
                )
                staged[component, row, cols - radius :] = base[cols - radius :] + scale * (
                    near[radius:] + far[cols - radius :]
                )
        copy = pltpu.make_async_copy(
            staged.at[:, pl.ds(start, group)], kicked.at[:, pl.ds(start, group)], sems.at[start // group]
        )
        copy.start()
        copies.append(copy)
    for copy in copies:
        copy.wait()


def call(body, outs, n_in, scratch=(), smem=(), far=(), near=(), kept=False, spaces=None, mib=8, cost=10**6):
    made = pl.pallas_call(
        body,
        out_shape=[
            pltpu.VMEM(s, d) if (kept if isinstance(kept, bool) else kept[at]) else jax.ShapeDtypeStruct(s, d)
            for at, (s, d) in enumerate(outs)
        ],
        in_specs=[SMEM if at in smem else HBM if at in far else VMEM for at in range(n_in)],
        out_specs=spaces or [VMEM for _ in outs],
        scratch_shapes=list(scratch),
        cost_estimate=pl.CostEstimate(flops=cost, bytes_accessed=cost, transcendentals=0),
        compiler_params=pltpu.CompilerParams(vmem_limit_bytes=mib * 1024 * 1024),
    )

    def run(*operands):
        return made(*[
            pltpu.with_memory_space_constraint(o, pltpu.HBM) if at in far
            else pltpu.with_memory_space_constraint(o, pltpu.VMEM) if at in near else o
            for at, o in enumerate(operands)
        ])

    return run


def per_device(density, momenta, smooth_taps, deriv_taps, kick_step):
    rows, cols, depth = density.shape
    radius = (smooth_taps.shape[0] - 1) // 2
    count_gx, count_gy = 2 * lax.axis_size("pair"), lax.axis_size("gy")
    assert rows == radius and cols >= 2 * radius and depth == LANES
    groups, lines, deep = rows // FACTOR, cols // FACTOR, depth // FACTOR
    assert groups == FACTOR and groups * deep == LANES
    coarse_x, coarse_y = groups * count_gx, lines * count_gy
    quads = coarse_x // groups
    assert quads % CHUNK == 0
    padded = -(-lines // 8) * 8
    f, b = jnp.float32, jnp.bfloat16

    basis_x, waves_x = real_basis(coarse_x)
    basis_y, waves_y = real_basis(coarse_y)
    basis_z, waves_z = real_basis(deep)

    pool = split_table(np.tile(np.repeat(basis_z.T, FACTOR, 0) / FACTOR**3, (1, groups)), 0)
    own, head, tail, coarse = call(
        prepare_kernel,
        [((rows, cols, depth), f), ((radius, rows, depth), f), ((radius, rows, depth), f), ((count_gx // 2 * count_gy, padded, LANES), f)],
        2,
        [pltpu.VMEM(pool.shape, b), pltpu.VMEM((groups * cols, depth), f), DMA((groups + 1,))], far=(0, 1),
        kept=(True, True, True, count_gx <= CHUNK),
    )(density, jnp.asarray(pool))

    def shift(values, pairs):
        return lax.ppermute(values, ("pair", "core", "gy"), [
            (a * count_gy + c, d * count_gy + e) for (a, c), (d, e) in pairs
        ])

    every = [(i, j) for i in range(count_gx) for j in range(count_gy)]
    beside = lambda i: i + 1 if i % 2 == 0 else i - 1
    across = lambda i: (i - 1) % count_gx if i % 2 == 0 else (i + 1) % count_gx
    crossed = shift(density, [((i, j), (across(i), j)) for i, j in every])
    swapped = shift(density, [((i, j), (beside(i), j)) for i, j in every])
    left = shift(tail, [((i, j), (i, (j + 1) % count_gy)) for i, j in every])
    right = shift(head, [((i, j), (i, (j - 1) % count_gy)) for i, j in every])
    cross_left = shift(tail, [((i, j), (across(i), (j + 1) % count_gy)) for i, j in every])
    cross_right = shift(head, [((i, j), (across(i), (j - 1) % count_gy)) for i, j in every])

    blocks = lax.all_to_all(coarse, ("pair", "gy"), split_axis=0, concat_axis=0, tiled=True)
    beside_blocks = shift(blocks, [((i, j), (beside(i), j)) for i, j in every])

    places = band_rows(rows, cols, depth, radius)
    bands, scale = call(
        functools.partial(bands_kernel, rows=rows, cols=cols, depth=depth, radius=radius),
        [((max(p[1] for p in places.values()), max(p[2] for p in places.values())), b), ((8, LANES), f)],
        3, [pltpu.SMEM(smooth_taps.shape, f), pltpu.SMEM(deriv_taps.shape, f), DMA((2,))], far=(0, 1), smem=(2,), kept=True,
    )(smooth_taps, deriv_taps, kick_step)

    spread = np.zeros((quads, count_gx, groups, groups, deep))
    for turn in range(groups):
        for j in range(groups):
            for quad in range(quads):
                spread[quad, :, turn, j, :] = basis_x[quad * groups + j].reshape(count_gx, groups)[
                    :, (j + turn) % groups
                ][:, None]
    back_y = np.concatenate([
        np.repeat(t.T.reshape(count_gy, lines, coarse_y), FACTOR, 1) for t in (basis_y, centred(basis_y))
    ], 1)
    back_x = np.stack([basis_x, centred(basis_x)])
    back_x = back_x.reshape(2, quads, groups, count_gx, groups).transpose(3, 1, 0, 4, 2)
    back_x = np.repeat(back_x[..., None], deep, -1).reshape(count_gx, -1, LANES)
    back_z = np.stack([
        np.tile(np.repeat(t, FACTOR, 1), (groups, 1)) * LONG_COUPLING for t in (basis_z, centred(basis_z))
    ])
    other = (eigenvalues(waves_x, coarse_x).reshape(quads, groups, 1) + eigenvalues(waves_z, deep)).reshape(
        quads, LANES
    )
    second = np.repeat(eigenvalues(waves_y, coarse_y)[:, None], LANES, 1)
    far_tables = [
        spread.reshape(-1, LANES).astype(np.float32),
        np.concatenate([second, other]).astype(np.float32), back_x.astype(np.float32),
        split_table(back_z, 1), split_table(basis_y, 1), split_table(back_y, 2),
    ]

    beside_left = shift(left, [((i, j), (beside(i), j)) for i, j in every])
    beside_right = shift(right, [((i, j), (beside(i), j)) for i, j in every])
    near_tables = [(t.shape[1:] if at in (2, 5) else t.shape, t.dtype) for at, t in enumerate(far_tables)]
    far_tables = [jnp.asarray(t) for t in far_tables]
    partial, *near_tables = call(
        functools.partial(inner_kernel, group=GROUP, radius=radius),
        [((3, rows, cols, depth), f)] + near_tables, 12,
        [pltpu.VMEM((rows * cols, depth), f), pltpu.VMEM((rows * cols, depth), f),
         pltpu.VMEM((3, rows, cols, depth), f), DMA, DMA((6,))],
        far=(4, 6, 7, 8, 9, 10, 11), near=(0, 1, 2, 3, 5), kept=(True,) + (count_gx <= CHUNK,) * 6,
        mib=8 if count_gx <= CHUNK else 52,
    )(own, swapped, crossed, bands, momenta, scale, *far_tables)
    (force,) = call(
        functools.partial(solve_kernel, lines=lines),
        [((3, groups, cols, depth), f)], 8,
        [pltpu.VMEM((coarse_y, CHUNK * LANES), f), pltpu.VMEM((coarse_x, coarse_y, LANES), f),
           pltpu.VMEM((quads, 2 * cols, LANES), f), pltpu.VMEM((3, groups * cols, LANES), f)],
        near=tuple(range(8)) if count_gx <= CHUNK else (), kept=count_gx <= CHUNK,
        mib=10 if count_gx <= CHUNK else 52,
    )(blocks, beside_blocks, *near_tables)
    (kicked,) = call(
        functools.partial(outer_kernel, group=GROUP),
        [((3, rows, cols, depth), f)], 10,
        [pltpu.VMEM((rows * 2 * radius, depth), f), pltpu.VMEM((rows * 2 * radius, depth), f),
         pltpu.VMEM((3, rows, cols, depth), f), DMA((rows // GROUP,))],
        near=tuple(range(10)), spaces=[HBM], mib=8,
    )(left, right, beside_left, beside_right, cross_left, cross_right, bands, partial, scale, force)
    return kicked


def solution(mesh):
    assert mesh.shape["gx"] % 2 == 0
    count_gx, count_gy = mesh.shape["gx"], mesh.shape["gy"]
    mesh = jax.sharding.Mesh(
        np.asarray(mesh.devices).reshape(count_gx // 2, 2, count_gy), ("pair", "core", "gy")
    )

    gx = ("pair", "core")
    in_specs = (P(gx, "gy", None), P(None, gx, "gy", None), P(), P(), P())
    out_specs = P(None, gx, "gy", None)
    return jax.shard_map(per_device, mesh=mesh, in_specs=in_specs, out_specs=out_specs, check_vma=False)
```

profile of v0, /device:TPU:0, one launch (start us, length us, event | category | flops | bytes accessed | tf_op | source)
XLA Modules:
  0.0 34.7 jit_solution(4403957666344623503)
XLA Ops:
  0.0 0.5 %collective-permute-start.6 = (f32[16,48,128]{2,1,0:T(8,128)}, f32[16,48,128]{2,1,0:T(8,128)S(1)}, u32[]{:S(2)}, u32[]{:S(2)}) collective-permute-start(f32[16,48,128]{2,1,0:T(8,128)} %density_far.1), channel_id=1, source_target_pairs={{0,4},{1,5},{2,6},{3,7},{4,0},{5,1},{6,2},{7,3},{8,12},{9,13},{10,... | collective-permute-start | bytes 1179656 | tf_op jit(solution)/shard_map/ppermute | solution.py:416
  0.5 4.7 %collective-permute-start.7 = (f32[16,48,128]{2,1,0:T(8,128)}, f32[16,48,128]{2,1,0:T(8,128)S(1)}, u32[]{:S(2)}, u32[]{:S(2)}) collective-permute-start(f32[16,48,128]{2,1,0:T(8,128)} %density_far.1), channel_id=1, source_target_pairs={{0,28},{1,29},{2,30},{3,31},{4,8},{5,9},{6,10},{7,11},{8,4},{9,5},... | collective-permute-start | bytes 1179656 | tf_op jit(solution)/shard_map/ppermute | solution.py:416
  5.2 2.0 %shard_map.118 = (f32[16,48,128]{2,1,0:T(8,128)S(1)}, f32[16,16,128]{2,1,0:T(8,128)S(1)}, f32[16,16,128]{2,1,0:T(8,128)S(1)}, f32[16,16,128]{2,1,0:T(8,128)}) custom-call(f32[16,48,128]{2,1,0:T(8,128)} %density_far.1, bf16[384,128]{1,0:T(8,128)(2,1)} %constant.14.clone.pool_far), custom_call_target="tpu_custom_call" | custom-call | flops 1000000 | bytes 1000000 | tf_op jit(solution)/shard_map/pallas_call | solution.py:380
  7.2 3.8 %all-to-all-start = ((f32[16,16,128]{2,1,0:T(8,128)}), f32[16,16,128]{2,1,0:T(8,128)S(1)}, u32[]{:S(2)}, u32[]{:S(2)}) async-start(f32[16,16,128]{2,1,0:T(8,128)} %get-tuple-element.24), calls=%async_computation | async-start | bytes 262144 | tf_op jit(solution)/shard_map/all_to_all | solution.py:430
  11.0 1.9 %collective-permute-start = (f32[16,16,128]{2,1,0:T(8,128)S(1)}, f32[16,16,128]{2,1,0:T(8,128)S(1)}, u32[]{:S(2)}, u32[]{:S(2)}) collective-permute-start(f32[16,16,128]{2,1,0:T(8,128)S(1)} %get-tuple-element.18), channel_id=1, source_target_pairs={{0,1},{1,2},{2,3},{3,0},{4,5},{5,6},{6,7},{7,4},{8,9},{9,10},{10,1... | collective-permute-start | bytes 393224 | tf_op jit(solution)/shard_map/ppermute | solution.py:416
  12.9 1.1 %collective-permute-start.1 = (f32[16,16,128]{2,1,0:T(8,128)S(1)}, f32[16,16,128]{2,1,0:T(8,128)S(1)}, u32[]{:S(2)}, u32[]{:S(2)}) collective-permute-start(f32[16,16,128]{2,1,0:T(8,128)S(1)} %get-tuple-element.19), channel_id=1, source_target_pairs={{0,3},{1,0},{2,1},{3,2},{4,7},{5,4},{6,5},{7,6},{8,11},{9,8},{10,9... | collective-permute-start | bytes 393224 | tf_op jit(solution)/shard_map/ppermute | solution.py:416
  14.0 5.2 %all-to-all-done.blocks = f32[16,16,128]{2,1,0:T(8,128)S(1)} async-done(((f32[16,16,128]{2,1,0:T(8,128)}), f32[16,16,128]{2,1,0:T(8,128)S(1)}, u32[]{:S(2)}, u32[]{:S(2)}) %all-to-all-start) | async-done | bytes 131104 | tf_op jit(solution)/shard_map/all_to_all | solution.py:430
  19.1 0.0 collective-permute-start.8
  19.2 0.6 %collective-permute-done.left = f32[16,16,128]{2,1,0:T(8,128)S(1)} collective-permute-done((f32[16,16,128]{2,1,0:T(8,128)S(1)}, f32[16,16,128]{2,1,0:T(8,128)S(1)}, u32[]{:S(2)}, u32[]{:S(2)}) %collective-permute-start) | collective-permute-done | bytes 131104 | tf_op jit(solution)/shard_map/ppermute | solution.py:416
  19.8 1.4 %collective-permute-start.4 = (f32[16,16,128]{2,1,0:T(8,128)S(1)}, f32[16,16,128]{2,1,0:T(8,128)S(1)}, u32[]{:S(2)}, u32[]{:S(2)}) collective-permute-start(f32[16,16,128]{2,1,0:T(8,128)S(1)} %get-tuple-element.18), channel_id=1, source_target_pairs={{0,29},{1,30},{2,31},{3,28},{4,9},{5,10},{6,11},{7,8},{8,5},{9,6},... | collective-permute-start | bytes 393224 | tf_op jit(solution)/shard_map/ppermute | solution.py:416
  21.2 0.1 collective-permute-done.1.right
  21.3 3.9 %collective-permute-start.5 = (f32[16,16,128]{2,1,0:T(8,128)S(1)}, f32[16,16,128]{2,1,0:T(8,128)S(1)}, u32[]{:S(2)}, u32[]{:S(2)}) collective-permute-start(f32[16,16,128]{2,1,0:T(8,128)S(1)} %get-tuple-element.19), channel_id=1, source_target_pairs={{0,31},{1,28},{2,29},{3,30},{4,11},{5,8},{6,9},{7,10},{8,7},{9,4},... | collective-permute-start | bytes 393224 | tf_op jit(solution)/shard_map/ppermute | solution.py:416
  25.1 0.0 collective-permute-done.6.swapped
  25.1 0.0 collective-permute-start.2
  25.2 0.0 collective-permute-done.7.crossed
  25.2 0.5 %collective-permute-start.3 = (f32[16,16,128]{2,1,0:T(8,128)S(1)}, f32[16,16,128]{2,1,0:T(8,128)S(1)}, u32[]{:S(2)}, u32[]{:S(2)}) collective-permute-start(f32[16,16,128]{2,1,0:T(8,128)S(1)} %collective-permute-done.1.right), channel_id=1, source_target_pairs={{0,4},{1,5},{2,6},{3,7},{4,0},{5,1},{6,2},{7,3},{8,12},{9,13},{10,... | collective-permute-start | bytes 393224 | tf_op jit(solution)/shard_map/ppermute | solution.py:416
  26.3 1.3 %shard_map.119 = (bf16[960,144]{1,0:T(8,128)(2,1)S(1)}, f32[8,128]{1,0:T(8,128)S(1)}) custom-call(f32[33]{0:T(128)} %smooth_far.1, f32[33]{0:T(128)} %deriv_far.1, f32[]{:T(128)S(6)} %copy.13.step), custom_call_target="tpu_custom_call" | custom-call | flops 1000000 | bytes 1000000 | tf_op jit(solution)/shard_map/pallas_call | solution.py:380
  27.6 3.5 %shard_map.120 = (f32[3,16,48,128]{3,2,1,0:T(8,128)S(1)}, f32[256,128]{1,0:T(8,128)S(1)}, f32[56,128]{1,0:T(8,128)S(1)}, f32[64,128]{1,0:T(8,128)S(1)}, bf16[2,3...) custom-call(f32[16,48,128]{2,1,0:T(8,128)S(1)} %get-tuple-element.21.own, ...), custom_call_target="tpu_custom_call" | custom-call | flops 1000000 | bytes 1000000 | tf_op jit(solution)/shard_map/pallas_call | solution.py:380
  31.1 0.0 collective-permute-done.8.beside_blocks
  31.1 1.3 %shard_map.121.force = f32[3,4,48,128]{3,2,1,0:T(8,128)S(1)} custom-call(f32[16,16,128]{2,1,0:T(8,128)S(1)} %all-to-all-done.blocks, f32[16,16,128]{2,1,0:T(8,128)S(1)} %collective-permute-done.8.beside_blocks, f32[256,128]{1,0:T(8,128)S(1)} %get-tuple-element.25.spread, f32[56,128]{1,0:T(8,128)S(1)} %get-tuple-element.26.tables, ...), custom_call_target="tpu_custom_call" | custom-call | flops 1000000 | bytes 1000000 | tf_op jit(solution)/shard_map/pallas_call | solution.py:380
  32.5 0.0 collective-permute-done.4.cross_left
  32.5 0.0 collective-permute-done.5.cross_right
  32.5 0.0 collective-permute-done.2.beside_left
  32.5 0.0 collective-permute-done.3.beside_right
  32.5 2.1 %shard_map.122 = f32[3,16,48,128]{3,2,1,0:T(8,128)} custom-call(f32[16,16,128]{2,1,0:T(8,128)S(1)} %collective-permute-done.left, f32[16,16,128]{2,1,0:T(8,128)S(1)} %collective-permute-done.1.right, f32[16,16,128]{2,1,0:T(8,128)S(1)} %collective-permute-done.2.beside_left, f32[16,16,128]{2,1,0:T(8,128)S(1)} %collective-permute-done.3.beside_right, ...), custom_call_target="tpu_custom_call" | custom-call | flops 1000000 | bytes 1000000 | tf_op jit(solution)/shard_map/pallas_call | solution.py:380
Async XLA Ops:
  0.0 25.1 %collective-permute-start.6 = (f32[16,48,128]{2,1,0:T(8,128)}, f32[16,48,128]{2,1,0:T(8,128)S(1)}, u32[]{:S(2)}, u32[]{:S(2)}) collective-permute-start(f32[16,48,128]{2,1,0:T(8,128)} %density_far.1), channel_id=1, source_target_pairs={{0,4},{1,5},{2,6},{3,7},{4,0},{5,1},{6,2},{7,3},{8,12},{9,13},{10,... | collective-permute-start | bytes 1179656 | tf_op jit(solution)/shard_map/ppermute | solution.py:416
  0.5 24.7 %collective-permute-start.7 = (f32[16,48,128]{2,1,0:T(8,128)}, f32[16,48,128]{2,1,0:T(8,128)S(1)}, u32[]{:S(2)}, u32[]{:S(2)}) collective-permute-start(f32[16,48,128]{2,1,0:T(8,128)} %density_far.1), channel_id=1, source_target_pairs={{0,28},{1,29},{2,30},{3,31},{4,8},{5,9},{6,10},{7,11},{8,4},{9,5},... | collective-permute-start | bytes 1179656 | tf_op jit(solution)/shard_map/ppermute | solution.py:416
  7.2 12.0 %all-to-all-start = ((f32[16,16,128]{2,1,0:T(8,128)}), f32[16,16,128]{2,1,0:T(8,128)S(1)}, u32[]{:S(2)}, u32[]{:S(2)}) async-start(f32[16,16,128]{2,1,0:T(8,128)} %get-tuple-element.24), calls=%async_computation | async-start | bytes 262144 | tf_op jit(solution)/shard_map/all_to_all | solution.py:430
  11.0 8.8 %collective-permute-start = (f32[16,16,128]{2,1,0:T(8,128)S(1)}, f32[16,16,128]{2,1,0:T(8,128)S(1)}, u32[]{:S(2)}, u32[]{:S(2)}) collective-permute-start(f32[16,16,128]{2,1,0:T(8,128)S(1)} %get-tuple-element.18), channel_id=1, source_target_pairs={{0,1},{1,2},{2,3},{3,0},{4,5},{5,6},{6,7},{7,4},{8,9},{9,10},{10,1... | collective-permute-start | bytes 393224 | tf_op jit(solution)/shard_map/ppermute | solution.py:416
  12.9 8.3 %collective-permute-start.1 = (f32[16,16,128]{2,1,0:T(8,128)S(1)}, f32[16,16,128]{2,1,0:T(8,128)S(1)}, u32[]{:S(2)}, u32[]{:S(2)}) collective-permute-start(f32[16,16,128]{2,1,0:T(8,128)S(1)} %get-tuple-element.19), channel_id=1, source_target_pairs={{0,3},{1,0},{2,1},{3,2},{4,7},{5,4},{6,5},{7,6},{8,11},{9,8},{10,9... | collective-permute-start | bytes 393224 | tf_op jit(solution)/shard_map/ppermute | solution.py:416
  19.1 12.0 %collective-permute-start.8 = (f32[16,16,128]{2,1,0:T(8,128)S(1)}, f32[16,16,128]{2,1,0:T(8,128)S(1)}, u32[]{:S(2)}, u32[]{:S(2)}) collective-permute-start(f32[16,16,128]{2,1,0:T(8,128)S(1)} %all-to-all-done.blocks), channel_id=1, source_target_pairs={{0,4},{1,5},{2,6},{3,7},{4,0},{5,1},{6,2},{7,3},{8,12},{9,13},{10,... | collective-permute-start | bytes 393224 | tf_op jit(solution)/shard_map/ppermute | solution.py:416
  19.8 12.7 %collective-permute-start.4 = (f32[16,16,128]{2,1,0:T(8,128)S(1)}, f32[16,16,128]{2,1,0:T(8,128)S(1)}, u32[]{:S(2)}, u32[]{:S(2)}) collective-permute-start(f32[16,16,128]{2,1,0:T(8,128)S(1)} %get-tuple-element.18), channel_id=1, source_target_pairs={{0,29},{1,30},{2,31},{3,28},{4,9},{5,10},{6,11},{7,8},{8,5},{9,6},... | collective-permute-start | bytes 393224 | tf_op jit(solution)/shard_map/ppermute | solution.py:416
  21.3 11.2 %collective-permute-start.5 = (f32[16,16,128]{2,1,0:T(8,128)S(1)}, f32[16,16,128]{2,1,0:T(8,128)S(1)}, u32[]{:S(2)}, u32[]{:S(2)}) collective-permute-start(f32[16,16,128]{2,1,0:T(8,128)S(1)} %get-tuple-element.19), channel_id=1, source_target_pairs={{0,31},{1,28},{2,29},{3,30},{4,11},{5,8},{6,9},{7,10},{8,7},{9,4},... | collective-permute-start | bytes 393224 | tf_op jit(solution)/shard_map/ppermute | solution.py:416
  25.1 7.3 %collective-permute-start.2 = (f32[16,16,128]{2,1,0:T(8,128)S(1)}, f32[16,16,128]{2,1,0:T(8,128)S(1)}, u32[]{:S(2)}, u32[]{:S(2)}) collective-permute-start(f32[16,16,128]{2,1,0:T(8,128)S(1)} %collective-permute-done.left), channel_id=1, source_target_pairs={{0,4},{1,5},{2,6},{3,7},{4,0},{5,1},{6,2},{7,3},{8,12},{9,13},{10,... | collective-permute-start | bytes 393224 | tf_op jit(solution)/shard_map/ppermute | solution.py:416
  25.2 7.3 %collective-permute-start.3 = (f32[16,16,128]{2,1,0:T(8,128)S(1)}, f32[16,16,128]{2,1,0:T(8,128)S(1)}, u32[]{:S(2)}, u32[]{:S(2)}) collective-permute-start(f32[16,16,128]{2,1,0:T(8,128)S(1)} %collective-permute-done.1.right), channel_id=1, source_target_pairs={{0,4},{1,5},{2,6},{3,7},{4,0},{5,1},{6,2},{7,3},{8,12},{9,13},{10,... | collective-permute-start | bytes 393224 | tf_op jit(solution)/shard_map/ppermute | solution.py:416
where the time goes:
time: 34.9 us; the launch traced here: 34.7 us
  starting transfers between devices  17.8 us (51%)
  Pallas kernels  10.2 us (29%)
  waiting for transfers between devices  5.88 us (17%)
  between operations  0.74 us (2%)
    ppermute x9, starting transfers between devices, shift(): lax.ppermute(values, ('pair', 'core', 'gy'), [(a * count_gy + c, d * coun...  14 us
    pallas_call x5, Pallas kernels, run(): made(*[pltpu.with_memory_space_constraint(o, pltpu.HBM) if at in far else...  10.2 us
    all_to_all x1, waiting for transfers between devices, per_device(): lax.all_to_all(coarse, ('pair', 'gy'), split_axis=0, concat_axis=0, tiled...  5.15 us
    all_to_all x1, starting transfers between devices, per_device(): lax.all_to_all(coarse, ('pair', 'gy'), split_axis=0, concat_axis=0, tiled...  3.84 us
    ppermute x9, waiting for transfers between devices, shift(): lax.ppermute(values, ('pair', 'core', 'gy'), [(a * count_gy + c, d * coun...  0.72 us
  transfers between devices with their start and end apart: 10, of which 3 were waited for; matrix products, arithmetic and copies ran while one was open for 0% of the time, Pallas kernels for 23%

commit v1 on v0

v1 whole, which is shorter than its diff:
```python
import functools
import math

import jax
import jax.numpy as jnp
import ml_dtypes
import numpy as np
from jax import lax
from jax.experimental import pallas as pl
from jax.experimental.pallas import tpu as pltpu
from jax.sharding import PartitionSpec as P


FACTOR = 4
LANES = 128
CHUNK = 8
GROUP = 16
SIDE_GROUP = 8
TILE = 4
LONG_COUPLING = 16.0
VMEM = pl.BlockSpec(memory_space=pltpu.VMEM)
SMEM = pl.BlockSpec(memory_space=pltpu.SMEM)
HBM = pl.BlockSpec(memory_space=pltpu.HBM)
DMA = pltpu.SemaphoreType.DMA


def real_basis(count):
    places = np.arange(count, dtype=np.float64)
    rows, waves = [np.full(count, 1.0 / math.sqrt(count))], [0]
    for wave in range(1, (count + 1) // 2):
        phase = 2.0 * math.pi * wave * places / count
        rows += [math.sqrt(2.0 / count) * np.cos(phase), math.sqrt(2.0 / count) * np.sin(phase)]
        waves += [wave, wave]
    if count % 2 == 0:
        rows.append(np.cos(math.pi * places) / math.sqrt(count))
        waves.append(count // 2)
    return np.stack(rows), np.array(waves)


def centred(basis):
    return 0.5 * (np.roll(basis, -1, 1) - np.roll(basis, 1, 1))


def eigenvalues(waves, count):
    return 2.0 - 2.0 * np.cos(2.0 * math.pi * waves / count)


def split_table(table, axis):
    table = np.asarray(table, dtype=np.float32)
    high = table.astype(ml_dtypes.bfloat16)
    low = (table - high.astype(np.float32)).astype(ml_dtypes.bfloat16)
    return np.concatenate([high, low, high], axis)


def split(values):
    high = values.astype(jnp.bfloat16)
    low = (values - high.astype(jnp.float32)).astype(jnp.bfloat16)
    return high, low


def tripled(values, axis):
    high, low = split(values)
    return jnp.concatenate([high, high, low], axis=axis)


def dot(left, right):
    return jnp.dot(left, right, preferred_element_type=jnp.float32)


def side_start(which, radius, cols):
    high = lax.axis_index("gy") % 2 == which
    return pl.multiple_of(jnp.where(high, cols - radius, 0), 16)


def prepare_kernel(
    density_far, pool_far, smooth_far, deriv_far, density, bands, strip_a_far, strip_b_far, coarse_far,
    coarse, pool_table, pooled, smooth, deriv, sems,
):
    rows, cols, depth = density.shape
    radius = strip_a_far.shape[1]
    groups, lines = rows // FACTOR, cols // FACTOR
    step = FACTOR
    copies = [
        pltpu.make_async_copy(
            density_far.at[pl.ds(step * group, step)], density.at[pl.ds(step * group, step)], sems.at[group]
        )
        for group in range(groups)
    ]
    for source, target in ((pool_far, pool_table), (smooth_far, smooth), (deriv_far, deriv)):
        copies.append(pltpu.make_async_copy(source, target, sems.at[len(copies)]))
    for copy in copies:
        copy.start()
    for group in range(groups):
        copies[group].wait()
        total = density[FACTOR * group]
        for at in range(1, FACTOR):
            total = total + density[FACTOR * group + at]
        pooled[group * cols : (group + 1) * cols, :] = total
    leaving = [
        pltpu.make_async_copy(
            density.at[:, pl.ds(side_start(which, radius, cols), radius)], target, sems.at[len(copies) + which]
        )
        for which, target in enumerate((strip_a_far, strip_b_far))
    ]
    for copy in leaving:
        copy.start()
    parts = []
    for group in range(groups):
        total = pooled[pl.ds(group * cols, lines, stride=FACTOR), :]
        for at in range(1, FACTOR):
            total = total + pooled[pl.ds(group * cols + at, lines, stride=FACTOR), :]
        parts.append(total)
    copies[groups].wait()
    waves = dot(tripled(jnp.concatenate(parts, axis=0), 1), pool_table[...])
    lane_group = lax.broadcasted_iota(jnp.int32, (lines, LANES), 1) // (LANES // groups)
    result = waves[:lines]
    for group in range(1, groups):
        result = jnp.where(lane_group == group, waves[group * lines : (group + 1) * lines], result)
    tiles = lines // TILE

    def spread_out(copy, carry):
        for tile in range(tiles):
            coarse[copy * tiles + tile] = result[tile * TILE : (tile + 1) * TILE]
        return carry

    lax.fori_loop(0, coarse.shape[0] // tiles, spread_out, 0, unroll=coarse.shape[0] <= 64)
    leaving.append(pltpu.make_async_copy(coarse, coarse_far, sems.at[len(copies) + 2]))
    leaving[-1].start()
    for copy in copies[groups + 1 :]:
        copy.wait()
    write_bands(smooth, deriv, bands, rows, cols, depth, radius)
    for copy in leaving:
        copy.wait()


def band_rows(rows, cols, depth, radius):
    sizes = {"x": (2 * rows, 3 * rows), "own": (2 * cols, cols), "smooth": (depth, depth), "deriv": (depth, depth)}
    sizes["sides"] = (4 * radius, 2 * radius)
    places, start = {}, 0
    for name, (height, width) in sizes.items():
        places[name] = (start, height, width)
        start += 2 * height
    return places, start


def band(bands, places, name):
    start, height, width = places[name]
    high = bands[start : start + height, :width]
    low = bands[start + height : start + 2 * height, :width]
    return jnp.concatenate([high, low, high], axis=0 if name in ("smooth", "deriv") else 1)


def write_bands(smooth, deriv, bands, rows, cols, depth, radius):
    taps = 2 * radius + 1
    odd = lax.axis_index("core")
    places, _ = band_rows(rows, cols, depth, radius)
    lane8 = lax.broadcasted_iota(jnp.int32, (8, LANES), 1)
    pair, turned_pair = [], []
    for weights in (smooth, deriv):
        row = turned = jnp.zeros((8, LANES), jnp.float32)
        for tap in range(taps):
            row = jnp.where(lane8 == tap, weights[tap], row)
            turned = jnp.where(lane8 == (LANES - tap) % LANES, weights[tap], turned)
        pair.append(row)
        turned_pair.append(turned)

    def toeplitz(row, height, shift):
        tall = jnp.concatenate([row] * (height // 8), axis=0)
        return pltpu.roll(tall, shift % LANES, 1, stride=1, stride_axis=0)

    def lanes_of(height):
        return lax.broadcasted_iota(jnp.int32, (height, LANES), 1)

    def write(name, matrix):
        high, low = split(matrix)
        start, height, _ = places[name]
        bands[start : start + height, :] = high
        bands[start + height : start + 2 * height, :] = low

    lane = lanes_of(rows)
    parts = []
    for row in pair:
        near = toeplitz(row, rows, -radius)
        later = jnp.where(lane < 2 * rows, near, toeplitz(row, rows, 2 * rows))
        earlier = jnp.where(
            lane < rows, near, jnp.where(lane < 2 * rows, toeplitz(row, rows, rows), toeplitz(row, rows, 0))
        )
        parts.append(jnp.where(odd == 1, earlier, later))
    write("x", jnp.concatenate(parts, axis=0))
    write("own", jnp.concatenate([toeplitz(row, cols, -radius) for row in pair], axis=0))
    lane, even = lanes_of(radius), lax.axis_index("gy") % 2 == 0
    parts = []
    for row in pair:
        nearer = jnp.where(even, toeplitz(row, radius, -2 * radius), toeplitz(row, radius, 0))
        other = jnp.where(even, toeplitz(row, radius, radius), toeplitz(row, radius, -radius))
        parts += [jnp.where(lane < radius, nearer, 0.0), jnp.where(lane < radius, 0.0, other)]
    write("sides", jnp.concatenate(parts, axis=0))
    for name, turned in zip(("smooth", "deriv"), turned_pair):
        write(name, toeplitz(turned, depth, radius))


def solve_kernel(
    blocks, beside_blocks, spread, tables, own_tables, back_z, forward, inverse, partial, scale_row, base,
    gathered, turned, back, columns, *, lines,
):
    core = lax.axis_index("core")
    rows, fine = partial.shape[1:3]
    groups = rows // FACTOR
    quads = back.shape[0]
    whole_y = gathered.shape[0]
    parts = whole_y // lines
    tiles = lines // TILE
    count = 2 * blocks.shape[0] // (parts * tiles)
    width = LANES // FACTOR
    few = count <= CHUNK

    def spin_block(pair, carry):
        for side, source in enumerate((blocks, beside_blocks)):
            for tile in range(parts * tiles):
                gathered[tile * TILE : (tile + 1) * TILE, :LANES] = source[pair * parts * tiles + tile]
            values = gathered[:, :LANES]
            place = (2 * pair + (core if side == 0 else 1 - core)) * FACTOR
            for spin in range(FACTOR):
                turned[place + spin] = values if spin == 0 else pltpu.roll(values, LANES - spin * width, 1)
        return carry

    lax.fori_loop(0, count // 2, spin_block, 0, unroll=few)

    def chunk(step, carry):
        for at in range(CHUNK):
            place = (step * CHUNK + at) * count * FACTOR

            def term(index, total):
                return total + turned[index] * spread[pl.ds(place + index, 1), :]

            gathered[:, at * LANES : (at + 1) * LANES] = lax.fori_loop(
                0, count * FACTOR, term, jnp.zeros((whole_y, LANES), jnp.float32), unroll=True if few else 4
            )
        values = dot(forward[...], tripled(gathered[...], 0))
        own = tables[:whole_y, :]
        total = jnp.concatenate(
            [own + tables[pl.ds(whole_y + step * CHUNK + at, 1), :] for at in range(CHUNK)], axis=1
        )
        scale = jnp.where(total > 0.0, 1.0 / jnp.where(total > 0.0, total, 1.0), 0.0)
        result = dot(inverse[...], tripled(values * scale, 0))
        for at in range(CHUNK):
            back[step * CHUNK + at] = result[:, at * LANES : (at + 1) * LANES]
        return carry

    lax.fori_loop(0, quads // CHUNK, chunk, 0)

    for group in range(groups):
        def collect(index, totals):
            whole = back[index]
            value, slope = whole[:fine], whole[fine:]
            along = own_tables[pl.ds(index * 2 * groups + group, 1), :]
            along_slope = own_tables[pl.ds((index * 2 + 1) * groups + group, 1), :]
            return (
                totals[0] + value * along_slope, totals[1] + slope * along, totals[2] + value * along,
            )

        zero = jnp.zeros((fine, LANES), jnp.float32)
        totals = lax.fori_loop(0, quads, collect, (zero, zero, zero), unroll=few)
        for component in range(3):
            columns[component, group * fine : (group + 1) * fine, :] = totals[component]
    for component in range(3):
        columns[component] = dot(tripled(columns[component], 1), back_z[1 if component == 2 else 0])
    scale = scale_row[0:1, :]
    for component in range(3):
        for row in range(rows):
            group = row // FACTOR
            far = columns[component, group * fine : (group + 1) * fine, :]
            base[component, row] = partial[component, row] + scale * far


def along_first(columns, matrix, smooth_x, deriv_x):
    rows, depth = matrix.shape[0] // 2, LANES
    for start in range(0, len(columns), CHUNK):
        some = columns[start : start + CHUNK]
        stacked = jnp.concatenate([tripled(jnp.concatenate(parts(), axis=0), 0) for parts in some], axis=1)
        result = dot(matrix, stacked)
        for at in range(len(some)):
            place = (start + at) * rows
            smooth_x[place : place + rows, :] = result[:rows, at * depth : (at + 1) * depth]
            deriv_x[place : place + rows, :] = result[rows:, at * depth : (at + 1) * depth]


def along_others(smooth_x, deriv_x, some, rows, wide, along_y, smooth_z, deriv_z):
    pieces = [[], [], []]
    count, depth = along_y.shape[0] // 2, LANES
    for row in some:
        values = jnp.concatenate([x[pl.ds(row, wide, stride=rows), :] for x in (smooth_x, deriv_x)], axis=1)
        result = dot(along_y, tripled(values, 0))
        for at, piece in enumerate((result[:count, depth:], result[count:, :depth], result[:count, :depth])):
            pieces[at].append(tripled(piece, 1))
    smooth = dot(jnp.concatenate(pieces[0] + pieces[1], axis=0), smooth_z)
    deriv = dot(jnp.concatenate(pieces[2], axis=0), deriv_z)
    number = len(some)
    return [
        [smooth[at * count : (at + 1) * count] for at in range(number)],
        [smooth[(number + at) * count : (number + at + 1) * count] for at in range(number)],
        [deriv[at * count : (at + 1) * count] for at in range(number)],
    ]


def load_kernel(
    spread_far, tables_far, own_tables_far, back_z_far, forward_far, inverse_far,
    spread, tables, own_tables, back_z, forward, inverse, sems,
):
    gx, gy = 2 * lax.axis_index("pair") + lax.axis_index("core"), lax.axis_index("gy")
    copies = [
        pltpu.make_async_copy(source, target, sems.at[at])
        for at, (source, target) in enumerate((
            (spread_far, spread), (tables_far, tables), (own_tables_far.at[gx], own_tables), (back_z_far, back_z),
            (forward_far, forward), (inverse_far.at[gy], inverse),
        ))
    ]
    for copy in copies:
        copy.start()
    for copy in copies:
        copy.wait()


def inner_kernel(
    own, swapped, crossed, bands, scale_row, momenta_far, partial, smooth_x, deriv_x, momenta, sems, *, group, radius
):
    _, rows, cols, depth = partial.shape
    arriving = [
        pltpu.make_async_copy(momenta_far.at[component], momenta.at[component], sems.at[component])
        for component in range(3)
    ]
    for copy in arriving:
        copy.start()
    places, _ = band_rows(rows, cols, depth, radius)
    along_x, own_y, smooth_z, deriv_z = [band(bands, places, n) for n in ("x", "own", "smooth", "deriv")]
    along_first(
        [lambda col=col: [x[pl.ds(col, rows, stride=cols), :] for x in (own, swapped, crossed)] for col in range(cols)],
        along_x, smooth_x, deriv_x,
    )
    for start in range(0, rows, group):
        short = along_others(
            smooth_x, deriv_x, range(start, start + group), rows, cols, own_y, smooth_z, deriv_z
        )
        for component in range(3):
            for at in range(group):
                partial[component, start + at] = short[component][at]
    scale = scale_row[0:1, :]
    for component in range(3):
        arriving[component].wait()
        for row in range(rows):
            partial[component, row] = momenta[component, row] + scale * partial[component, row]


def cut_kernel(tile, strip):
    radius = strip.shape[1]
    strip[...] = tile[:, pl.ds(side_start(1, radius, tile.shape[1]), radius), :]


def outer_kernel(
    strip_a, strip_b, beside_a, beside_b, cross_a, cross_b, bands, scale_row, base, kicked,
    smooth_x, deriv_x, staged, sems, *, group,
):
    _, rows, cols, depth = base.shape
    radius = strip_a.shape[0] // rows
    places, _ = band_rows(rows, cols, depth, radius)
    along_x, along_y, smooth_z, deriv_z = [band(bands, places, n) for n in ("x", "sides", "smooth", "deriv")]
    along_first(
        [
            lambda col=col, blocks=blocks: [x[pl.ds(col, rows, stride=radius), :] for x in blocks]
            for blocks in ((strip_a, beside_a, cross_a), (strip_b, beside_b, cross_b)) for col in range(radius)
        ],
        along_x, smooth_x, deriv_x,
    )
    scale = scale_row[0:1, :]
    copies = []
    for start in range(0, rows, group):
        short = along_others(
            smooth_x, deriv_x, range(start, start + group), rows, 2 * radius, along_y, smooth_z, deriv_z
        )
        for component in range(3):
            for at in range(group):
                row = start + at
                staged[component, row, radius : cols - radius] = base[component, row, radius : cols - radius]
                for which in range(2):
                    side = pl.ds(side_start(which, radius, cols), radius)
                    near = short[component][at][which * radius : (which + 1) * radius]
                    staged[component, row, side] = base[component, row, side] + scale * near
        copies.append(pltpu.make_async_copy(
            staged.at[:, pl.ds(start, group)], kicked.at[:, pl.ds(start, group)], sems.at[start // group]
        ))
        copies[-1].start()
    for copy in copies:
        copy.wait()


def call(body, outs, n_in, scratch=(), smem=(), far=(), near=(), kept=False, spaces=None, mib=8, cost=10**6, alias={}):
    made = pl.pallas_call(
        body,
        out_shape=[
            pltpu.VMEM(s, d) if (kept if isinstance(kept, bool) else kept[at]) else jax.ShapeDtypeStruct(s, d)
            for at, (s, d) in enumerate(outs)
        ],
        in_specs=[SMEM if at in smem else HBM if at in far else VMEM for at in range(n_in)],
        out_specs=spaces or [VMEM for _ in outs],
        scratch_shapes=list(scratch),
        input_output_aliases=alias,
        cost_estimate=pl.CostEstimate(flops=cost, bytes_accessed=cost, transcendentals=0),
        compiler_params=pltpu.CompilerParams(vmem_limit_bytes=mib * 1024 * 1024),
    )

    def run(*operands):
        return made(*[
            pltpu.with_memory_space_constraint(o, pltpu.HBM) if at in far
            else pltpu.with_memory_space_constraint(o, pltpu.VMEM) if at in near else o
            for at, o in enumerate(operands)
        ])

    return run


def per_device(density, momenta, smooth_taps, deriv_taps, kick_step):
    rows, cols, depth = density.shape
    radius = (smooth_taps.shape[0] - 1) // 2
    count_gx, count_gy = 2 * lax.axis_size("pair"), lax.axis_size("gy")
    assert count_gy % 2 == 0 and radius % 16 == 0
    assert rows == radius and cols >= 2 * radius and depth == LANES
    groups, lines, deep = rows // FACTOR, cols // FACTOR, depth // FACTOR
    assert groups == FACTOR and groups * deep == LANES
    coarse_x, coarse_y = groups * count_gx, lines * count_gy
    quads = coarse_x // groups
    assert quads % CHUNK == 0
    assert lines % TILE == 0
    f, b = jnp.float32, jnp.bfloat16

    basis_x, waves_x = real_basis(coarse_x)
    basis_y, waves_y = real_basis(coarse_y)
    basis_z, waves_z = real_basis(deep)

    pool = split_table(np.tile(np.repeat(basis_z.T, FACTOR, 0) / FACTOR**3, (1, groups)), 0)
    _, band_height = band_rows(rows, cols, depth, radius)
    own, bands, send_a, send_b, coarse = call(
        prepare_kernel,
        [((rows, cols, depth), f), ((band_height, LANES), b), ((rows, radius, depth), f), ((rows, radius, depth), f),
         ((count_gx // 2 * count_gy * (lines // TILE), TILE, LANES), f)],
        4,
        [pltpu.VMEM((count_gx // 2 * count_gy * (lines // TILE), TILE, LANES), f), pltpu.VMEM(pool.shape, b),
         pltpu.VMEM((groups * cols, depth), f), pltpu.SMEM(smooth_taps.shape, f), pltpu.SMEM(deriv_taps.shape, f),
         DMA((groups + 6,))],
        far=(0, 1, 2, 3), kept=(True, True, False, False, False), spaces=[VMEM, VMEM, HBM, HBM, HBM],
        mib=8 if count_gx <= CHUNK else 24,
    )(density, jnp.asarray(pool), smooth_taps, deriv_taps)

    def shift(values, pairs):
        return lax.ppermute(values, ("pair", "core", "gy"), [
            (a * count_gy + c, d * count_gy + e) for (a, c), (d, e) in pairs
        ])

    every = [(i, j) for i in range(count_gx) for j in range(count_gy)]
    beside = lambda i: i + 1 if i % 2 == 0 else i - 1
    across = lambda i: (i - 1) % count_gx if i % 2 == 0 else (i + 1) % count_gx
    crossed = shift(density, [((i, j), (across(i), j)) for i, j in every])
    swapped = shift(density, [((i, j), (beside(i), j)) for i, j in every])
    pair_a = lambda j: j + 1 if j % 2 == 0 else j - 1
    pair_b = lambda j: (j + 1) % count_gy if j % 2 == 1 else (j - 1) % count_gy
    strip_a = shift(send_a, [((i, j), (i, pair_a(j))) for i, j in every])
    strip_b = shift(send_b, [((i, j), (i, pair_b(j))) for i, j in every])
    cross_a = shift(strip_a, [((i, j), (across(i), j)) for i, j in every])
    (crossed_b,) = call(cut_kernel, [((rows, radius, depth), f)], 1, near=(0,), kept=True)(crossed)
    cross_b = shift(crossed_b, [((i, j), (i, pair_b(j))) for i, j in every])

    blocks = lax.all_to_all(coarse, ("pair", "gy"), split_axis=0, concat_axis=0, tiled=True)
    beside_blocks = shift(blocks, [((i, j), (beside(i), j)) for i, j in every])

    scale = jnp.broadcast_to(kick_step, (8, LANES))
    spread = np.zeros((quads, count_gx, groups, groups, deep))
    for turn in range(groups):
        for j in range(groups):
            for quad in range(quads):
                spread[quad, :, turn, j, :] = basis_x[quad * groups + j].reshape(count_gx, groups)[
                    :, (j + turn) % groups
                ][:, None]
    back_y = np.concatenate([
        np.repeat(t.T.reshape(count_gy, lines, coarse_y), FACTOR, 1) for t in (basis_y, centred(basis_y))
    ], 1)
    back_x = np.stack([basis_x, centred(basis_x)])
    back_x = back_x.reshape(2, quads, groups, count_gx, groups).transpose(3, 1, 0, 4, 2)
    back_x = np.repeat(back_x[..., None], deep, -1).reshape(count_gx, -1, LANES)
    back_z = np.stack([
        np.tile(np.repeat(t, FACTOR, 1), (groups, 1)) * LONG_COUPLING for t in (basis_z, centred(basis_z))
    ])
    other = (eigenvalues(waves_x, coarse_x).reshape(quads, groups, 1) + eigenvalues(waves_z, deep)).reshape(
        quads, LANES
    )
    second = np.repeat(eigenvalues(waves_y, coarse_y)[:, None], LANES, 1)
    far_tables = [
        spread.reshape(-1, LANES).astype(np.float32),
        np.concatenate([second, other]).astype(np.float32), back_x.astype(np.float32),
        split_table(back_z, 1), split_table(basis_y, 1), split_table(back_y, 2),
    ]

    beside_a = shift(strip_a, [((i, j), (beside(i), j)) for i, j in every])
    beside_b = shift(strip_b, [((i, j), (beside(i), j)) for i, j in every])
    near_tables = [(t.shape[1:] if at in (2, 5) else t.shape, t.dtype) for at, t in enumerate(far_tables)]
    far_tables = [jnp.asarray(t) for t in far_tables]
    small = count_gx <= CHUNK
    near_tables = call(
        load_kernel, near_tables, 6, [DMA((6,))], far=tuple(range(6)), kept=small, mib=8 if small else 52,
    )(*far_tables)
    (partial,) = call(
        functools.partial(inner_kernel, group=GROUP, radius=radius),
        [((3, rows, cols, depth), f)], 6,
        [pltpu.VMEM((rows * cols, depth), f), pltpu.VMEM((rows * cols, depth), f),
         pltpu.VMEM((3, rows, cols, depth), f), DMA((3,))],
        far=(5,), near=(0, 1, 2, 3, 4), kept=True,
    )(*[x.reshape(rows * cols, depth) for x in (own, swapped, crossed)], bands, scale, momenta)
    (base,) = call(
        functools.partial(solve_kernel, lines=lines),
        [((3, rows, cols, depth), f)], 10,
        [pltpu.VMEM((coarse_y, CHUNK * LANES), f), pltpu.VMEM((coarse_x, coarse_y, LANES), f),
         pltpu.VMEM((quads, 2 * cols, LANES), f), pltpu.VMEM((3, groups * cols, LANES), f)],
        near=tuple(range(10)) if small else (), kept=small, mib=8 if small else 52, alias={8: 0},
    )(blocks, beside_blocks, *near_tables, partial, scale)
    strips = [x.reshape(rows * radius, depth) for x in (strip_a, strip_b, beside_a, beside_b, cross_a, cross_b)]
    (kicked,) = call(
        functools.partial(outer_kernel, group=SIDE_GROUP), [((3, rows, cols, depth), f)], 9,
        [pltpu.VMEM((2 * rows * radius, depth), f), pltpu.VMEM((2 * rows * radius, depth), f),
         pltpu.VMEM((3, rows, cols, depth), f), DMA((rows // SIDE_GROUP,))],
        near=tuple(range(9)), spaces=[HBM],
    )(*strips, bands, scale, base)
    return kicked


def solution(mesh):
    assert mesh.shape["gx"] % 2 == 0
    count_gx, count_gy = mesh.shape["gx"], mesh.shape["gy"]
    mesh = jax.sharding.Mesh(
        np.asarray(mesh.devices).reshape(count_gx // 2, 2, count_gy), ("pair", "core", "gy")
    )

    gx = ("pair", "core")
    in_specs = (P(gx, "gy", None), P(None, gx, "gy", None), P(), P(), P())
    out_specs = P(None, gx, "gy", None)
    return jax.shard_map(per_device, mesh=mesh, in_specs=in_specs, out_specs=out_specs, check_vma=False)
```

time: 34.9 us -> 31.6 us (0.905)
  waiting for transfers between devices: 5.88 us -> 3.96 us
  Pallas kernels: 10.2 us -> 8.41 us
  starting transfers between devices: 17.8 us -> 18.2 us
    all_to_all x1, waiting for transfers between devices: 5.15 us -> 0.01 us  [per_device(): lax.all_to_all(coarse, ('pair', 'gy'), split_axis=0, concat_axis=0, tiled...]
    ppermute x9, waiting for transfers between devices: 0.72 us -> 3.96 us  [shift(): lax.ppermute(values, ('pair', 'core', 'gy'), [(a * count_gy + c, d * coun...]
    pallas_call x5 -> x6, Pallas kernels: 10.2 us -> 8.41 us  [run(): made(*[pltpu.with_memory_space_constraint(o, pltpu.HBM) if at in far else...]
    all_to_all x1, starting transfers between devices: 3.84 us -> 4.51 us  [per_device(): lax.all_to_all(coarse, ('pair', 'gy'), split_axis=0, concat_axis=0, tiled...]
  transfers between devices with their start and end apart: 10 -> 10, of which waited for: 3 -> 1; matrix products, arithmetic and copies ran while one was open for 0% -> 0% of each run, Pallas kernels for 23% -> 20%
where the time goes in v1:
time: 31.6 us; the launch traced here: 31.3 us
  starting transfers between devices  18.2 us (58%)
  Pallas kernels  8.41 us (27%)
  waiting for transfers between devices  3.96 us (13%)
  between operations  0.76 us (2%)
    ppermute x9, starting transfers between devices, shift(): lax.ppermute(values, ('pair', 'core', 'gy'), [(a * count_gy + c, d * coun...  13.7 us
    pallas_call x6, Pallas kernels, run(): made(*[pltpu.with_memory_space_constraint(o, pltpu.HBM) if at in far else...  8.41 us
    all_to_all x1, starting transfers between devices, per_device(): lax.all_to_all(coarse, ('pair', 'gy'), split_axis=0, concat_axis=0, tiled...  4.51 us
    ppermute x9, waiting for transfers between devices, shift(): lax.ppermute(values, ('pair', 'core', 'gy'), [(a * count_gy + c, d * coun...  3.96 us
  transfers between devices with their start and end apart: 10, of which 1 were waited for; matrix products, arithmetic and copies ran while one was open for 0% of the time, Pallas kernels for 20%

profile of v1, /device:TPU:0, one launch (start us, length us, event | category | flops | bytes accessed | tf_op | source)
XLA Modules:
  0.0 31.3 jit_solution(1947831570016259744)
XLA Ops:
  0.0 4.5 %collective-permute-start.5 = (f32[16,48,128]{2,1,0:T(8,128)}, f32[16,48,128]{2,1,0:T(8,128)S(1)}, u32[]{:S(2)}, u32[]{:S(2)}) collective-permute-start(f32[16,48,128]{2,1,0:T(8,128)} %density_far.1), channel_id=1, source_target_pairs={{0,28},{1,29},{2,30},{3,31},{4,8},{5,9},{6,10},{7,11},{8,4},{9,5},... | collective-permute-start | bytes 1179656 | tf_op jit(solution)/shard_map/ppermute | solution.py:454
  4.5 0.0 collective-permute-start.8
  4.5 2.0 %shard_map.118 = (f32[16,48,128]{2,1,0:T(8,128)S(1)}, bf16[896,128]{1,0:T(8,128)(2,1)S(1)}, f32[16,16,128]{2,1,0:T(8,128)S(1)}, f32[16,16,128]{2,1,0:T(8,128)S(1)}, f32[48,4,128]{2,1,0:T(4,128)}) custom-call(f32[16,48,128]{2,1,0:T(8,128)} %density_far.1, bf16[384,128]{1,0:T(8,128)(2,1)} %constant.14.clone.pool_far, f32[33]{0:T(128)} %smooth_far.1, f32[33]{0:T(128)} %deriv_far.1), custom_call_target="tpu_custom_call" | custom-call | flops 1000000 | bytes 1000000 | tf_op jit(solution)/shard_map/pallas_call | solution.py:412
  6.5 4.5 %all-to-all-start = ((f32[48,4,128]{2,1,0:T(4,128)}), f32[48,4,128]{2,1,0:T(4,128)S(1)}, u32[]{:S(2)}, u32[]{:S(2)}) async-start(f32[48,4,128]{2,1,0:T(4,128)} %get-tuple-element.19), calls=%async_computation | async-start | bytes 196608 | tf_op jit(solution)/shard_map/all_to_all | solution.py:471
  11.0 1.9 %collective-permute-start = (f32[16,16,128]{2,1,0:T(8,128)S(1)}, f32[16,16,128]{2,1,0:T(8,128)S(1)}, u32[]{:S(2)}, u32[]{:S(2)}) collective-permute-start(f32[16,16,128]{2,1,0:T(8,128)S(1)} %get-tuple-element.16), channel_id=1, source_target_pairs={{0,1},{1,0},{2,3},{3,2},{4,5},{5,4},{6,7},{7,6},{8,9},{9,8},{10,11... | collective-permute-start | bytes 393224 | tf_op jit(solution)/shard_map/ppermute | solution.py:454
  12.9 1.5 %collective-permute-start.1 = (f32[16,16,128]{2,1,0:T(8,128)S(1)}, f32[16,16,128]{2,1,0:T(8,128)S(1)}, u32[]{:S(2)}, u32[]{:S(2)}) collective-permute-start(f32[16,16,128]{2,1,0:T(8,128)S(1)} %get-tuple-element.17), channel_id=1, source_target_pairs={{0,3},{1,2},{2,1},{3,0},{4,7},{5,6},{6,5},{7,4},{8,11},{9,10},{10,... | collective-permute-start | bytes 393224 | tf_op jit(solution)/shard_map/ppermute | solution.py:454
  14.4 3.9 %collective-permute-done = f32[16,16,128]{2,1,0:T(8,128)S(1)} collective-permute-done((f32[16,16,128]{2,1,0:T(8,128)S(1)}, f32[16,16,128]{2,1,0:T(8,128)S(1)}, u32[]{:S(2)}, u32[]{:S(2)}) %collective-permute-start) | collective-permute-done | bytes 131104 | tf_op jit(solution)/shard_map/ppermute | solution.py:454
  18.3 0.0 collective-permute-start.2
  18.3 3.5 %collective-permute-start.4 = (f32[16,16,128]{2,1,0:T(8,128)S(1)}, f32[16,16,128]{2,1,0:T(8,128)S(1)}, u32[]{:S(2)}, u32[]{:S(2)}) collective-permute-start(f32[16,16,128]{2,1,0:T(8,128)S(1)} %collective-permute-done), channel_id=1, source_target_pairs={{0,28},{1,29},{2,30},{3,31},{4,8},{5,9},{6,10},{7,11},{8,4},{9,5},... | collective-permute-start | bytes 393224 | tf_op jit(solution)/shard_map/ppermute | solution.py:454
  21.8 0.0 collective-permute-done.1
  21.8 0.0 collective-permute-start.3
  21.8 0.0 collective-permute-done.5.tile
  21.8 2.1 %collective-permute-start.6 = (f32[16,16,128]{2,1,0:T(8,128)S(1)}, f32[16,16,128]{2,1,0:T(8,128)S(1)}, u32[]{:S(2)}, u32[]{:S(2)}) collective-permute-start(f32[16,16,128]{2,1,0:T(8,128)S(1)} %shard_map.119), channel_id=1, source_target_pairs={{0,3},{1,2},{2,1},{3,0},{4,7},{5,6},{6,5},{7,4},{8,11},{9,10},{10,... | collective-permute-start | bytes 393224 | tf_op jit(solution)/shard_map/ppermute | solution.py:454
  23.9 0.0 all-to-all-done.blocks
  23.9 0.0 collective-permute-done.8
  23.9 0.2 collective-permute-start.7
  24.8 1.1 %shard_map.120 = (f32[256,128]{1,0:T(8,128)S(1)}, f32[56,128]{1,0:T(8,128)S(1)}, f32[64,128]{1,0:T(8,128)S(1)}, bf16[2,384,128]{2,1,0:T(8,128)(2,1)S(1)}, bf16[4...) custom-call(f32[256,128]{1,0:T(8,128)} %constant.15.clone.spread_far, f32[56,128]{1,0:T(8,128)} %constant.16.clone.tables_far, ...), custom_call_target="tpu_custom_call" | custom-call | flops 1000000 | bytes 1000000 | tf_op jit(solution)/shard_map/pallas_call | solution.py:412
  25.9 1.8 %shard_map.121.partial = f32[3,16,48,128]{3,2,1,0:T(8,128)S(1)} custom-call(f32[768,128]{1,0:T(8,128)S(1)} %bitcast.11, f32[768,128]{1,0:T(8,128)S(1)} %bitcast.10, f32[768,128]{1,0:T(8,128)S(1)} %bitcast.9, bf16[896,128]{1,0:T(8,128)(2,1)S(1)} %get-tuple-element.18.bands, f32[8,128]{1,0:T(8,128)S(1)} %broadcast_in_dim.3.scale_row, ...), custom_call_target="tpu_custom_call" | custom-call | flops 1000000 | bytes 1000000 | tf_op jit(solution)/shard_map/pallas_call | solution.py:412
  27.7 0.0 collective-permute-done.7.beside_blocks
  27.7 1.4 %shard_map.122.base = f32[3,16,48,128]{3,2,1,0:T(8,128)S(1)} custom-call(f32[48,4,128]{2,1,0:T(4,128)S(1)} %all-to-all-done.blocks, f32[48,4,128]{2,1,0:T(4,128)S(1)} %collective-permute-done.7.beside_blocks, f32[256,128]{1,0:T(8,128)S(1)} %get-tuple-element.20.spread, f32[56,128]{1,0:T(8,128)S(1)} %get-tuple-element.21.tables, ...), custom_call_target="tpu_custom_call", output_to_operand_aliasing={{}: (8, {})} | custom-call | flops 1000000 | bytes 1000000 | tf_op jit(solution)/shard_map/pallas_call | solution.py:412
  29.1 0.0 collective-permute-done.2
  29.2 0.0 collective-permute-done.4
  29.2 0.0 collective-permute-done.3
  29.2 0.0 collective-permute-done.6
  29.2 2.1 %shard_map.123 = f32[3,16,48,128]{3,2,1,0:T(8,128)} custom-call(f32[256,128]{1,0:T(8,128)S(1)} %bitcast.12, f32[256,128]{1,0:T(8,128)S(1)} %bitcast.13, f32[256,128]{1,0:T(8,128)S(1)} %bitcast.14, f32[256,128]{1,0:T(8,128)S(1)} %bitcast.16, f32[256,128]{1,0:T(8,128)S(1)} %bitcast.15, f32[256,128]{1,0:T(8,128)S(1)} %bitcast.17, ...), custom_call_target="tpu_custom_call" | custom-call | flops 1000000 | bytes 1000000 | tf_op jit(solution)/shard_map/pallas_call | solution.py:412
  (2 shorter events, 0.0 us)
Async XLA Ops:
  0.0 21.8 %collective-permute-start.5 = (f32[16,48,128]{2,1,0:T(8,128)}, f32[16,48,128]{2,1,0:T(8,128)S(1)}, u32[]{:S(2)}, u32[]{:S(2)}) collective-permute-start(f32[16,48,128]{2,1,0:T(8,128)} %density_far.1), channel_id=1, source_target_pairs={{0,28},{1,29},{2,30},{3,31},{4,8},{5,9},{6,10},{7,11},{8,4},{9,5},... | collective-permute-start | bytes 1179656 | tf_op jit(solution)/shard_map/ppermute | solution.py:454
  4.5 19.4 %collective-permute-start.8 = (f32[16,48,128]{2,1,0:T(8,128)}, f32[16,48,128]{2,1,0:T(8,128)S(1)}, u32[]{:S(2)}, u32[]{:S(2)}) collective-permute-start(f32[16,48,128]{2,1,0:T(8,128)} %density_far.1), channel_id=1, source_target_pairs={{0,4},{1,5},{2,6},{3,7},{4,0},{5,1},{6,2},{7,3},{8,12},{9,13},{10,... | collective-permute-start | bytes 1179656 | tf_op jit(solution)/shard_map/ppermute | solution.py:454
  6.5 17.4 %all-to-all-start = ((f32[48,4,128]{2,1,0:T(4,128)}), f32[48,4,128]{2,1,0:T(4,128)S(1)}, u32[]{:S(2)}, u32[]{:S(2)}) async-start(f32[48,4,128]{2,1,0:T(4,128)} %get-tuple-element.19), calls=%async_computation | async-start | bytes 196608 | tf_op jit(solution)/shard_map/all_to_all | solution.py:471
  11.0 7.3 %collective-permute-start = (f32[16,16,128]{2,1,0:T(8,128)S(1)}, f32[16,16,128]{2,1,0:T(8,128)S(1)}, u32[]{:S(2)}, u32[]{:S(2)}) collective-permute-start(f32[16,16,128]{2,1,0:T(8,128)S(1)} %get-tuple-element.16), channel_id=1, source_target_pairs={{0,1},{1,0},{2,3},{3,2},{4,5},{5,4},{6,7},{7,6},{8,9},{9,8},{10,11... | collective-permute-start | bytes 393224 | tf_op jit(solution)/shard_map/ppermute | solution.py:454
  12.9 8.9 %collective-permute-start.1 = (f32[16,16,128]{2,1,0:T(8,128)S(1)}, f32[16,16,128]{2,1,0:T(8,128)S(1)}, u32[]{:S(2)}, u32[]{:S(2)}) collective-permute-start(f32[16,16,128]{2,1,0:T(8,128)S(1)} %get-tuple-element.17), channel_id=1, source_target_pairs={{0,3},{1,2},{2,1},{3,0},{4,7},{5,6},{6,5},{7,4},{8,11},{9,10},{10,... | collective-permute-start | bytes 393224 | tf_op jit(solution)/shard_map/ppermute | solution.py:454
  18.3 10.8 %collective-permute-start.2 = (f32[16,16,128]{2,1,0:T(8,128)S(1)}, f32[16,16,128]{2,1,0:T(8,128)S(1)}, u32[]{:S(2)}, u32[]{:S(2)}) collective-permute-start(f32[16,16,128]{2,1,0:T(8,128)S(1)} %collective-permute-done), channel_id=1, source_target_pairs={{0,4},{1,5},{2,6},{3,7},{4,0},{5,1},{6,2},{7,3},{8,12},{9,13},{10,... | collective-permute-start | bytes 393224 | tf_op jit(solution)/shard_map/ppermute | solution.py:454
  18.3 10.8 %collective-permute-start.4 = (f32[16,16,128]{2,1,0:T(8,128)S(1)}, f32[16,16,128]{2,1,0:T(8,128)S(1)}, u32[]{:S(2)}, u32[]{:S(2)}) collective-permute-start(f32[16,16,128]{2,1,0:T(8,128)S(1)} %collective-permute-done), channel_id=1, source_target_pairs={{0,28},{1,29},{2,30},{3,31},{4,8},{5,9},{6,10},{7,11},{8,4},{9,5},... | collective-permute-start | bytes 393224 | tf_op jit(solution)/shard_map/ppermute | solution.py:454
  21.8 7.4 %collective-permute-start.3 = (f32[16,16,128]{2,1,0:T(8,128)S(1)}, f32[16,16,128]{2,1,0:T(8,128)S(1)}, u32[]{:S(2)}, u32[]{:S(2)}) collective-permute-start(f32[16,16,128]{2,1,0:T(8,128)S(1)} %collective-permute-done.1), channel_id=1, source_target_pairs={{0,4},{1,5},{2,6},{3,7},{4,0},{5,1},{6,2},{7,3},{8,12},{9,13},{10,... | collective-permute-start | bytes 393224 | tf_op jit(solution)/shard_map/ppermute | solution.py:454
  21.8 7.3 %collective-permute-start.6 = (f32[16,16,128]{2,1,0:T(8,128)S(1)}, f32[16,16,128]{2,1,0:T(8,128)S(1)}, u32[]{:S(2)}, u32[]{:S(2)}) collective-permute-start(f32[16,16,128]{2,1,0:T(8,128)S(1)} %shard_map.119), channel_id=1, source_target_pairs={{0,3},{1,2},{2,1},{3,0},{4,7},{5,6},{6,5},{7,4},{8,11},{9,10},{10,... | collective-permute-start | bytes 393224 | tf_op jit(solution)/shard_map/ppermute | solution.py:454
  23.9 3.8 %collective-permute-start.7 = (f32[48,4,128]{2,1,0:T(4,128)S(1)}, f32[48,4,128]{2,1,0:T(4,128)S(1)}, u32[]{:S(2)}, u32[]{:S(2)}) collective-permute-start(f32[48,4,128]{2,1,0:T(4,128)S(1)} %all-to-all-done.blocks), channel_id=1, source_target_pairs={{0,4},{1,5},{2,6},{3,7},{4,0},{5,1},{6,2},{7,3},{8,12},{9,13},{10,... | collective-permute-start | bytes 294920 | tf_op jit(solution)/shard_map/ppermute | solution.py:454

commit v2 on v1

--- a/solution.py
+++ b/solution.py
@@ -303,6 +303,11 @@
     ]
 
 
+def join_kernel(first, second, both):
+    both[: first.shape[0]] = first[...]
+    both[first.shape[0] :] = second[...]
+
+
 def load_kernel(
     spread_far, tables_far, own_tables_far, back_z_far, forward_far, inverse_far,
     spread, tables, own_tables, back_z, forward, inverse, sems,
@@ -357,7 +362,7 @@
 
 
 def outer_kernel(
-    strip_a, strip_b, beside_a, beside_b, cross_a, cross_b, bands, scale_row, base, kicked,
+    strip_a, strip_b, besides, cross_a, cross_b, bands, scale_row, base, kicked,
     smooth_x, deriv_x, staged, sems, *, group,
 ):
     _, rows, cols, depth = base.shape
@@ -366,8 +371,12 @@
     along_x, along_y, smooth_z, deriv_z = [band(bands, places, n) for n in ("x", "sides", "smooth", "deriv")]
     along_first(
         [
-            lambda col=col, blocks=blocks: [x[pl.ds(col, rows, stride=radius), :] for x in blocks]
-            for blocks in ((strip_a, beside_a, cross_a), (strip_b, beside_b, cross_b)) for col in range(radius)
+            lambda start=start, col=col, strip=strip, cross=cross: [
+                strip[pl.ds(col, rows, stride=radius), :], besides[pl.ds(start + col, rows, stride=radius), :],
+                cross[pl.ds(col, rows, stride=radius), :],
+            ]
+            for start, strip, cross in ((0, strip_a, cross_a), (rows * radius, strip_b, cross_b))
+            for col in range(radius)
         ],
         along_x, smooth_x, deriv_x,
     )
@@ -498,8 +507,8 @@
         split_table(back_z, 1), split_table(basis_y, 1), split_table(back_y, 2),
     ]
 
-    beside_a = shift(strip_a, [((i, j), (beside(i), j)) for i, j in every])
-    beside_b = shift(strip_b, [((i, j), (beside(i), j)) for i, j in every])
+    (joined,) = call(join_kernel, [((2 * rows, radius, depth), f)], 2, near=(0, 1), kept=True)(strip_a, strip_b)
+    besides = shift(joined, [((i, j), (beside(i), j)) for i, j in every])
     near_tables = [(t.shape[1:] if at in (2, 5) else t.shape, t.dtype) for at, t in enumerate(far_tables)]
     far_tables = [jnp.asarray(t) for t in far_tables]
     small = count_gx <= CHUNK
@@ -520,12 +529,12 @@
          pltpu.VMEM((quads, 2 * cols, LANES), f), pltpu.VMEM((3, groups * cols, LANES), f)],
         near=tuple(range(10)) if small else (), kept=small, mib=8 if small else 52, alias={8: 0},
     )(blocks, beside_blocks, *near_tables, partial, scale)
-    strips = [x.reshape(rows * radius, depth) for x in (strip_a, strip_b, beside_a, beside_b, cross_a, cross_b)]
+    strips = [x.reshape(-1, depth) for x in (strip_a, strip_b, besides, cross_a, cross_b)]
     (kicked,) = call(
-        functools.partial(outer_kernel, group=SIDE_GROUP), [((3, rows, cols, depth), f)], 9,
+        functools.partial(outer_kernel, group=SIDE_GROUP), [((3, rows, cols, depth), f)], 8,
         [pltpu.VMEM((2 * rows * radius, depth), f), pltpu.VMEM((2 * rows * radius, depth), f),
          pltpu.VMEM((3, rows, cols, depth), f), DMA((rows // SIDE_GROUP,))],
-        near=tuple(range(9)), spaces=[HBM],
+        near=tuple(range(8)), spaces=[HBM],
     )(*strips, bands, scale, base)
     return kicked
 

time: 31.6 us -> 28.3 us (0.90)
  starting transfers between devices: 18.2 us -> 14.3 us
  waiting for transfers between devices: 3.96 us -> 4.58 us
    ppermute x9 -> x8, starting transfers between devices: 13.7 us -> 10.7 us  [shift(): lax.ppermute(values, ('pair', 'core', 'gy'), [(a * count_gy + c, d * coun...]
    all_to_all x1, waiting for transfers between devices: 0.01 us -> 1.36 us  [per_device(): lax.all_to_all(coarse, ('pair', 'gy'), split_axis=0, concat_axis=0, tiled...]
    all_to_all x1, starting transfers between devices: 4.51 us -> 3.55 us  [per_device(): lax.all_to_all(coarse, ('pair', 'gy'), split_axis=0, concat_axis=0, tiled...]
    ppermute x9 -> x8, waiting for transfers between devices: 3.96 us -> 3.21 us  [shift(): lax.ppermute(values, ('pair', 'core', 'gy'), [(a * count_gy + c, d * coun...]
    pallas_call x6 -> x7, Pallas kernels: 8.41 us -> 8.45 us  [run(): made(*[pltpu.with_memory_space_constraint(o, pltpu.HBM) if at in far else...]
  transfers between devices with their start and end apart: 10 -> 9, of which waited for: 1 -> 2; matrix products, arithmetic and copies ran while one was open for 0% -> 0% of each run, Pallas kernels for 20% -> 23%
where the time goes in v2:
time: 28.3 us; the launch traced here: 28.1 us
  starting transfers between devices  14.3 us (51%)
  Pallas kernels  8.45 us (30%)
  waiting for transfers between devices  4.58 us (16%)
  between operations  0.77 us (3%)
    ppermute x8, starting transfers between devices, shift(): lax.ppermute(values, ('pair', 'core', 'gy'), [(a * count_gy + c, d * coun...  10.7 us
    pallas_call x7, Pallas kernels, run(): made(*[pltpu.with_memory_space_constraint(o, pltpu.HBM) if at in far else...  8.45 us
    all_to_all x1, starting transfers between devices, per_device(): lax.all_to_all(coarse, ('pair', 'gy'), split_axis=0, concat_axis=0, tiled...  3.55 us
    ppermute x8, waiting for transfers between devices, shift(): lax.ppermute(values, ('pair', 'core', 'gy'), [(a * count_gy + c, d * coun...  3.21 us
    all_to_all x1, waiting for transfers between devices, per_device(): lax.all_to_all(coarse, ('pair', 'gy'), split_axis=0, concat_axis=0, tiled...  1.36 us
  transfers between devices with their start and end apart: 9, of which 2 were waited for; matrix products, arithmetic and copies ran while one was open for 0% of the time, Pallas kernels for 23%

profile of v2, /device:TPU:0, one launch (start us, length us, event | category | flops | bytes accessed | tf_op | source)
XLA Modules:
  0.0 28.1 jit_solution(6956674222262048975)
XLA Ops:
  0.0 4.5 %collective-permute-start.4 = (f32[16,48,128]{2,1,0:T(8,128)}, f32[16,48,128]{2,1,0:T(8,128)S(1)}, u32[]{:S(2)}, u32[]{:S(2)}) collective-permute-start(f32[16,48,128]{2,1,0:T(8,128)} %density_far.1), channel_id=1, source_target_pairs={{0,28},{1,29},{2,30},{3,31},{4,8},{5,9},{6,10},{7,11},{8,4},{9,5},... | collective-permute-start | bytes 1179656 | tf_op jit(solution)/shard_map/ppermute | solution.py:463
  4.5 0.0 collective-permute-start.7
  4.5 2.0 %shard_map.118 = (f32[16,48,128]{2,1,0:T(8,128)S(1)}, bf16[896,128]{1,0:T(8,128)(2,1)S(1)}, f32[16,16,128]{2,1,0:T(8,128)S(1)}, f32[16,16,128]{2,1,0:T(8,128)S(1)}, f32[48,4,128]{2,1,0:T(4,128)}) custom-call(f32[16,48,128]{2,1,0:T(8,128)} %density_far.1, bf16[384,128]{1,0:T(8,128)(2,1)} %constant.14.clone.pool_far, f32[33]{0:T(128)} %smooth_far.1, f32[33]{0:T(128)} %deriv_far.1), custom_call_target="tpu_custom_call" | custom-call | flops 1000000 | bytes 1000000 | tf_op jit(solution)/shard_map/pallas_call | solution.py:421
  6.5 1.6 %collective-permute-start = (f32[16,16,128]{2,1,0:T(8,128)S(1)}, f32[16,16,128]{2,1,0:T(8,128)S(1)}, u32[]{:S(2)}, u32[]{:S(2)}) collective-permute-start(f32[16,16,128]{2,1,0:T(8,128)S(1)} %get-tuple-element.16), channel_id=1, source_target_pairs={{0,1},{1,0},{2,3},{3,2},{4,5},{5,4},{6,7},{7,6},{8,9},{9,8},{10,11... | collective-permute-start | bytes 393224 | tf_op jit(solution)/shard_map/ppermute | solution.py:463
  8.0 1.5 %collective-permute-start.1 = (f32[16,16,128]{2,1,0:T(8,128)S(1)}, f32[16,16,128]{2,1,0:T(8,128)S(1)}, u32[]{:S(2)}, u32[]{:S(2)}) collective-permute-start(f32[16,16,128]{2,1,0:T(8,128)S(1)} %get-tuple-element.17), channel_id=1, source_target_pairs={{0,3},{1,2},{2,1},{3,0},{4,7},{5,6},{6,5},{7,4},{8,11},{9,10},{10,... | collective-permute-start | bytes 393224 | tf_op jit(solution)/shard_map/ppermute | solution.py:463
  9.5 3.5 %all-to-all-start = ((f32[48,4,128]{2,1,0:T(4,128)}), f32[48,4,128]{2,1,0:T(4,128)S(1)}, u32[]{:S(2)}, u32[]{:S(2)}) async-start(f32[48,4,128]{2,1,0:T(4,128)} %get-tuple-element.19), calls=%async_computation | async-start | bytes 196608 | tf_op jit(solution)/shard_map/all_to_all | solution.py:480
  13.1 0.0 collective-permute-done.first
  13.1 3.2 %collective-permute-done.1.second = f32[16,16,128]{2,1,0:T(8,128)S(1)} collective-permute-done((f32[16,16,128]{2,1,0:T(8,128)S(1)}, f32[16,16,128]{2,1,0:T(8,128)S(1)}, u32[]{:S(2)}, u32[]{:S(2)}) %collective-permute-start.1) | collective-permute-done | bytes 131104 | tf_op jit(solution)/shard_map/ppermute | solution.py:463
  16.3 0.1 collective-permute-start.2
  16.4 0.6 %collective-permute-start.3 = (f32[16,16,128]{2,1,0:T(8,128)S(1)}, f32[16,16,128]{2,1,0:T(8,128)S(1)}, u32[]{:S(2)}, u32[]{:S(2)}) collective-permute-start(f32[16,16,128]{2,1,0:T(8,128)S(1)} %collective-permute-done.first), channel_id=1, source_target_pairs={{0,28},{1,29},{2,30},{3,31},{4,8},{5,9},{6,10},{7,11},{8,4},{9,5},... | collective-permute-start | bytes 393224 | tf_op jit(solution)/shard_map/ppermute | solution.py:463
  17.0 0.0 collective-permute-done.4.tile
  17.1 2.4 %collective-permute-start.5 = (f32[16,16,128]{2,1,0:T(8,128)S(1)}, f32[16,16,128]{2,1,0:T(8,128)S(1)}, u32[]{:S(2)}, u32[]{:S(2)}) collective-permute-start(f32[16,16,128]{2,1,0:T(8,128)S(1)} %shard_map.120), channel_id=1, source_target_pairs={{0,3},{1,2},{2,1},{3,0},{4,7},{5,6},{6,5},{7,4},{8,11},{9,10},{10,... | collective-permute-start | bytes 393224 | tf_op jit(solution)/shard_map/ppermute | solution.py:463
  19.5 1.4 %all-to-all-done.blocks = f32[48,4,128]{2,1,0:T(4,128)S(1)} async-done(((f32[48,4,128]{2,1,0:T(4,128)}), f32[48,4,128]{2,1,0:T(4,128)S(1)}, u32[]{:S(2)}, u32[]{:S(2)}) %all-to-all-start) | async-done | bytes 98336 | tf_op jit(solution)/shard_map/all_to_all | solution.py:480
  20.9 0.0 collective-permute-start.6
  21.5 1.1 %shard_map.121 = (f32[256,128]{1,0:T(8,128)S(1)}, f32[56,128]{1,0:T(8,128)S(1)}, f32[64,128]{1,0:T(8,128)S(1)}, bf16[2,384,128]{2,1,0:T(8,128)(2,1)S(1)}, bf16[4...) custom-call(f32[256,128]{1,0:T(8,128)} %constant.15.clone.spread_far, f32[56,128]{1,0:T(8,128)} %constant.16.clone.tables_far, ...), custom_call_target="tpu_custom_call" | custom-call | flops 1000000 | bytes 1000000 | tf_op jit(solution)/shard_map/pallas_call | solution.py:421
  22.6 0.0 collective-permute-done.7
  22.6 1.8 %shard_map.122.partial = f32[3,16,48,128]{3,2,1,0:T(8,128)S(1)} custom-call(f32[768,128]{1,0:T(8,128)S(1)} %bitcast.12, f32[768,128]{1,0:T(8,128)S(1)} %bitcast.11, f32[768,128]{1,0:T(8,128)S(1)} %bitcast.8, bf16[896,128]{1,0:T(8,128)(2,1)S(1)} %get-tuple-element.18.bands, f32[8,128]{1,0:T(8,128)S(1)} %broadcast_in_dim.3.scale_row, ...), custom_call_target="tpu_custom_call" | custom-call | flops 1000000 | bytes 1000000 | tf_op jit(solution)/shard_map/pallas_call | solution.py:421
  24.5 0.0 collective-permute-done.6.beside_blocks
  24.5 1.4 %shard_map.123.base = f32[3,16,48,128]{3,2,1,0:T(8,128)S(1)} custom-call(f32[48,4,128]{2,1,0:T(4,128)S(1)} %all-to-all-done.blocks, f32[48,4,128]{2,1,0:T(4,128)S(1)} %collective-permute-done.6.beside_blocks, f32[256,128]{1,0:T(8,128)S(1)} %get-tuple-element.20.spread, f32[56,128]{1,0:T(8,128)S(1)} %get-tuple-element.21.tables, ...), custom_call_target="tpu_custom_call", output_to_operand_aliasing={{}: (8, {})} | custom-call | flops 1000000 | bytes 1000000 | tf_op jit(solution)/shard_map/pallas_call | solution.py:421
  25.9 0.0 collective-permute-done.3
  25.9 0.0 collective-permute-done.2
  25.9 0.0 collective-permute-done.5
  25.9 2.1 %shard_map.124 = f32[3,16,48,128]{3,2,1,0:T(8,128)} custom-call(f32[256,128]{1,0:T(8,128)S(1)} %bitcast.9, f32[256,128]{1,0:T(8,128)S(1)} %bitcast.10, f32[512,128]{1,0:T(8,128)S(1)} %bitcast.13, f32[256,128]{1,0:T(8,128)S(1)} %bitcast.14, f32[256,128]{1,0:T(8,128)S(1)} %bitcast.15, bf16[896,128]{1,0:T(8,128)(2,1)S(1)} %get-tuple-element.18.bands, ...), custom_call_target="tpu_custom_call" | custom-call | flops 1000000 | bytes 1000000 | tf_op jit(solution)/shard_map/pallas_call | solution.py:421
  (3 shorter events, 0.0 us)
Async XLA Ops:
  0.0 17.0 %collective-permute-start.4 = (f32[16,48,128]{2,1,0:T(8,128)}, f32[16,48,128]{2,1,0:T(8,128)S(1)}, u32[]{:S(2)}, u32[]{:S(2)}) collective-permute-start(f32[16,48,128]{2,1,0:T(8,128)} %density_far.1), channel_id=1, source_target_pairs={{0,28},{1,29},{2,30},{3,31},{4,8},{5,9},{6,10},{7,11},{8,4},{9,5},... | collective-permute-start | bytes 1179656 | tf_op jit(solution)/shard_map/ppermute | solution.py:463
  4.5 18.1 %collective-permute-start.7 = (f32[16,48,128]{2,1,0:T(8,128)}, f32[16,48,128]{2,1,0:T(8,128)S(1)}, u32[]{:S(2)}, u32[]{:S(2)}) collective-permute-start(f32[16,48,128]{2,1,0:T(8,128)} %density_far.1), channel_id=1, source_target_pairs={{0,4},{1,5},{2,6},{3,7},{4,0},{5,1},{6,2},{7,3},{8,12},{9,13},{10,... | collective-permute-start | bytes 1179656 | tf_op jit(solution)/shard_map/ppermute | solution.py:463
  6.5 6.6 %collective-permute-start = (f32[16,16,128]{2,1,0:T(8,128)S(1)}, f32[16,16,128]{2,1,0:T(8,128)S(1)}, u32[]{:S(2)}, u32[]{:S(2)}) collective-permute-start(f32[16,16,128]{2,1,0:T(8,128)S(1)} %get-tuple-element.16), channel_id=1, source_target_pairs={{0,1},{1,0},{2,3},{3,2},{4,5},{5,4},{6,7},{7,6},{8,9},{9,8},{10,11... | collective-permute-start | bytes 393224 | tf_op jit(solution)/shard_map/ppermute | solution.py:463
  8.0 8.2 %collective-permute-start.1 = (f32[16,16,128]{2,1,0:T(8,128)S(1)}, f32[16,16,128]{2,1,0:T(8,128)S(1)}, u32[]{:S(2)}, u32[]{:S(2)}) collective-permute-start(f32[16,16,128]{2,1,0:T(8,128)S(1)} %get-tuple-element.17), channel_id=1, source_target_pairs={{0,3},{1,2},{2,1},{3,0},{4,7},{5,6},{6,5},{7,4},{8,11},{9,10},{10,... | collective-permute-start | bytes 393224 | tf_op jit(solution)/shard_map/ppermute | solution.py:463
  9.5 11.3 %all-to-all-start = ((f32[48,4,128]{2,1,0:T(4,128)}), f32[48,4,128]{2,1,0:T(4,128)S(1)}, u32[]{:S(2)}, u32[]{:S(2)}) async-start(f32[48,4,128]{2,1,0:T(4,128)} %get-tuple-element.19), calls=%async_computation | async-start | bytes 196608 | tf_op jit(solution)/shard_map/all_to_all | solution.py:480
  16.3 9.6 %collective-permute-start.2 = (f32[32,16,128]{2,1,0:T(8,128)S(1)}, f32[32,16,128]{2,1,0:T(8,128)S(1)}, u32[]{:S(2)}, u32[]{:S(2)}) collective-permute-start(f32[32,16,128]{2,1,0:T(8,128)S(1)} %shard_map.119), channel_id=1, source_target_pairs={{0,4},{1,5},{2,6},{3,7},{4,0},{5,1},{6,2},{7,3},{8,12},{9,13},{10,... | collective-permute-start | bytes 786440 | tf_op jit(solution)/shard_map/ppermute | solution.py:463
  16.4 9.5 %collective-permute-start.3 = (f32[16,16,128]{2,1,0:T(8,128)S(1)}, f32[16,16,128]{2,1,0:T(8,128)S(1)}, u32[]{:S(2)}, u32[]{:S(2)}) collective-permute-start(f32[16,16,128]{2,1,0:T(8,128)S(1)} %collective-permute-done.first), channel_id=1, source_target_pairs={{0,28},{1,29},{2,30},{3,31},{4,8},{5,9},{6,10},{7,11},{8,4},{9,5},... | collective-permute-start | bytes 393224 | tf_op jit(solution)/shard_map/ppermute | solution.py:463
  17.1 8.9 %collective-permute-start.5 = (f32[16,16,128]{2,1,0:T(8,128)S(1)}, f32[16,16,128]{2,1,0:T(8,128)S(1)}, u32[]{:S(2)}, u32[]{:S(2)}) collective-permute-start(f32[16,16,128]{2,1,0:T(8,128)S(1)} %shard_map.120), channel_id=1, source_target_pairs={{0,3},{1,2},{2,1},{3,0},{4,7},{5,6},{6,5},{7,4},{8,11},{9,10},{10,... | collective-permute-start | bytes 393224 | tf_op jit(solution)/shard_map/ppermute | solution.py:463
  20.9 3.6 %collective-permute-start.6 = (f32[48,4,128]{2,1,0:T(4,128)S(1)}, f32[48,4,128]{2,1,0:T(4,128)S(1)}, u32[]{:S(2)}, u32[]{:S(2)}) collective-permute-start(f32[48,4,128]{2,1,0:T(4,128)S(1)} %all-to-all-done.blocks), channel_id=1, source_target_pairs={{0,4},{1,5},{2,6},{3,7},{4,0},{5,1},{6,2},{7,3},{8,12},{9,13},{10,... | collective-permute-start | bytes 294920 | tf_op jit(solution)/shard_map/ppermute | solution.py:463
